TPU v7x, 256 devices: a whole 4x4x8 slice. The times are simulated.
256 devices in a mesh: cuts: 4 (over x), region: 64 (over z, y, core).
Axes of the slice: x: 4, y: 4, z: 8, core: 2. Of those that a mesh axis runs over, the one named last changes fastest.
Arguments:
- image: float32 [4096, 64, 128], P('region', 'cuts'), may hold values from -6 to 6
- precond: float32 [4096, 64, 128], P('region', 'cuts'), may hold values from 1 to 4
- table: bfloat16 [32, 4, 128, 128], replicated, may hold values from 0 to 0.019897461
- subset: int32 [32], replicated, may hold values from 0 to 31, each once
- tile_pixel: int32 [64, 2048], P('region'), may hold values from 0 to 63
- tile_slot: int32 [64, 2048], P('region'), may hold values from 0 to 127
- send_count: int32 [64, 64], P('region'), may hold values from 1 to 5, 128 in all within a row
- recv_map: int32 [64, 64, 5], replicated, may hold values from 0 to 5
- measured: float32 [384, 64, 128], P('region', 'cuts'), may hold values from -6 to 6
- stat_weight: float32 [384, 64, 128], P('region', 'cuts'), may hold values from 0.25 to 1
Outputs:
- updated: float32 [4096, 64, 128], P('region', 'cuts')
- residual: float32 [384, 64, 128], P('region', 'cuts')
Inputs may be any that keep to these rules, and one draw needn't show every extreme that they name: `send_count`: each row sums to 128; a region's slots are laid out by owner, in owner order. `recv_map`: entry [d, r, p] is used only where p < send_count[r, d]. `subset`: A permutation of the 32 tabulated angles.
All inputs are finite; a program needn't handle non-finite values.
Results may differ from a plain program's by a relative error of at most 0.005.
Values may be sent and summed in bfloat16 or wider, within the bound.
No kernel may reach another device: no remote copies, remote signals or barrier semaphores. Data moves between devices by JAX's collectives and lax.ppermute only.
A program may use at most 128 MiB of HBM per device.

v0:
```python
import jax
import jax.numpy as jnp
from jax import lax
from jax.sharding import PartitionSpec as P

ANG = 16
SHIFTS = 4
OWN = 6
CAP = 5


smoothing_weight = 0.5


def extended(cells, sides, width):
    for axis, dim in sides:
        count = lax.axis_size(axis)
        ends = count - 1
        head = lax.slice_in_dim(cells, 0, width, axis=dim)
        tail = lax.slice_in_dim(cells, cells.shape[dim] - width, cells.shape[dim], axis=dim)
        cells = jnp.concatenate(
            [
                lax.ppermute(tail, axis, [(i, (i + 1) % count) for i in range(ends)]),
                cells,
                lax.ppermute(head, axis, [((i + 1) % count, i) for i in range(ends)]),
            ],
            axis=dim,
        )
    return cells


def pick_rows(indices, count, source):
    selector = (indices[:, None] == jnp.arange(count, dtype=jnp.int32)[None, :]).astype(
        jnp.bfloat16
    )
    flat = source.reshape(count, -1)
    picked = jnp.dot(selector, flat, preferred_element_type=jnp.float32).astype(jnp.bfloat16)
    return picked.reshape((indices.shape[0],) + source.shape[1:])


def sum_rows(indices, count, source):
    selector = (jnp.arange(count, dtype=jnp.int32)[:, None] == indices[None, :]).astype(jnp.float32)
    flat = source.reshape(indices.shape[0], -1)
    summed = jnp.dot(
        selector, flat, preferred_element_type=jnp.float32, precision=lax.Precision.HIGHEST
    )
    return summed.reshape((count,) + source.shape[1:])


def per_device(
    image,
    precond,
    table,
    subset,
    tile_pixel,
    tile_slot,
    send_count,
    recv_map,
    measured,
    stat_weight,
):
    blocks = image.shape[0]
    slabs = image.shape[1]
    tile_width = image.shape[2]
    regions = lax.axis_size("region")
    slot_total = 2 * regions
    myself = lax.axis_index("region")
    tile_pixels = tile_pixel[0]
    tile_slots = tile_slot[0]
    footprints = jnp.take(table, subset[:ANG], axis=0).reshape(ANG * SHIFTS, tile_width, tile_width)
    gathered = pick_rows(tile_pixels, blocks, image.astype(jnp.bfloat16))
    gathered = gathered.reshape(ANG * SHIFTS, blocks // 2, slabs, tile_width)
    partial_value = jnp.einsum(
        "kij,ktsj->ktsi", footprints, gathered, preferred_element_type=jnp.float32
    )
    partial_value = partial_value.reshape(-1, slabs, tile_width)
    local_sums = sum_rows(tile_slots, slot_total, partial_value)
    counts = send_count[0]
    slot_ends = jnp.cumsum(counts)
    starts = slot_ends - counts
    slot_index = jnp.arange(slot_total, dtype=jnp.int32)
    target = jnp.sum((slot_ends[None, :] <= slot_index[:, None]).astype(jnp.int32), axis=1)
    position = slot_index - starts[target]
    lane_index = jnp.arange(CAP, dtype=jnp.int32)
    source_rows = (starts[:, None] + lane_index[None, :]).reshape(-1)
    filled = (lane_index[None, :] < counts[:, None]).reshape(-1)
    chooser = ((source_rows[:, None] == slot_index[None, :]) & filled[:, None]).astype(jnp.float32)
    outgoing = jnp.dot(
        chooser,
        local_sums.reshape(slot_total, -1),
        preferred_element_type=jnp.float32,
        precision=lax.Precision.HIGHEST,
    )
    outgoing = outgoing.reshape(regions, CAP, slabs, tile_width)
    incoming = lax.all_to_all(
        outgoing.astype(jnp.bfloat16), "region", split_axis=0, concat_axis=0, tiled=True
    ).astype(outgoing.dtype)
    owned_map = lax.dynamic_index_in_dim(recv_map, myself, 0, keepdims=False).reshape(-1)
    summed = sum_rows(owned_map, OWN, incoming.reshape(-1, slabs, tile_width))
    residual = stat_weight * (measured - summed)
    resid_half = residual.astype(jnp.bfloat16)
    returning = pick_rows(owned_map, OWN, resid_half).reshape(regions, CAP, slabs, tile_width)
    answers = lax.all_to_all(returning, "region", split_axis=0, concat_axis=0, tiled=True)
    slot_place = target * CAP + position
    slot_resid = pick_rows(
        slot_place, regions * CAP, answers.reshape(regions * CAP, slabs, tile_width)
    )
    tile_resid = pick_rows(tile_slots, slot_total, slot_resid).reshape(
        ANG * SHIFTS, blocks // 2, slabs, tile_width
    )
    back_terms = jnp.einsum(
        "kij,ktsi->ktsj", footprints, tile_resid, preferred_element_type=jnp.float32
    )
    gradient = sum_rows(tile_pixels, blocks, back_terms.reshape(-1, slabs, tile_width))
    padded = extended(image, (("cuts", 1),), 1)
    global_slice = lax.axis_index("cuts") * slabs + jnp.arange(slabs, dtype=jnp.int32)
    slab_total = slabs * lax.axis_size("cuts")
    below = jnp.where((global_slice > 0)[None, :, None], image - padded[:, :-2, :], 0.0)
    above = jnp.where((global_slice < slab_total - 1)[None, :, None], image - padded[:, 2:, :], 0.0)
    smooth = below + above
    updated = image + (gradient - smoothing_weight * smooth) / precond
    return (updated, residual)


def solution(mesh):
    in_specs = (
        P("region", "cuts", None),
        P("region", "cuts", None),
        P(),
        P(),
        P("region", None),
        P("region", None),
        P("region", None),
        P(),
        P("region", "cuts", None),
        P("region", "cuts", None),
    )
    out_specs = (P("region", "cuts", None), P("region", "cuts", None))
    return jax.shard_map(
        per_device, mesh=mesh, in_specs=in_specs, out_specs=out_specs, check_vma=False
    )
```

profile of v0, /device:TPU:1, one launch (start us, length us, event | category | flops | bytes accessed | tf_op | source)
XLA Modules:
  0.0 217.5 jit_solution(12343083902011778841)
XLA Ops:
  0.6 0.0 copy-start
  0.6 0.7 compare_and_fusion
  1.4 0.1 broadcast_in_dim.51
  1.4 0.1 broadcast_in_dim.52
  1.5 1.1 convert_element_type.37
  2.6 5.3 %convert_bitcast_fusion.1 = bf16[256,8,16,128]{3,1,2,0:T(8,128)(2,1)} fusion(s32[2048]{0:T(1024)} %bitcast.105, bf16[8,8,16,128]{3,2,1,0:T(8,128)(2,1)S(1)} %bitcast.104), kind=kOutput, calls=%fused_computation.11 | convolution fusion | flops 541196288 | bytes 8658944 | tf_op jit(solution)/shard_map/dot_general | solution.py:37
  7.9 9.8 %copy.61 = bf16[256,8,16,128]{3,2,1,0:T(8,128)(2,1)} copy(bf16[256,8,16,128]{3,1,2,0:T(8,128)(2,1)} %convert_bitcast_fusion.1) | data formatting | bytes 16777216
  17.7 0.1 copy.42
  17.8 0.1 reduce-window.7
  17.9 0.1 reduce
  18.0 0.1 iota_add_fusion
  18.1 0.1 add.76
  18.2 0.1 iota_compare_fusion.13
  18.3 0.2 lt.51
  18.5 4.3 %gather_fusion.1 = bf16[16,4,128,128]{3,2,1,0:T(8,128)(2,1)} fusion(bf16[32,4,128,128]{3,2,1,0:T(8,128)(2,1)} %param.12, s32[1024]{0:T(1024)S(1)} %pad_clamp_fusion), kind=kCustom, calls=%fused_computation.1 | custom fusion | bytes 4194368 | tf_op jit(solution)/shard_map/jit(_take)/gather | solution.py:70
  22.8 1.8 bitcast_select_fusion
  24.6 0.0 copy-start.5
  24.7 11.5 %fusion.5 = f32[64,32,16,128]{3,2,1,0:T(8,128)} fusion(bf16[64,128,128]{2,1,0:T(8,128)(2,1)S(1)} %bitcast_select_fusion, bf16[64,32,16,128]{3,2,1,0:T(8,128)(2,1)} %bitcast.100), kind=kOutput, calls=%fused_computation.8 | convolution fusion | flops 1073741824 | bytes 27262976 | tf_op jit(solution)/shard_map/kij,ktsj->ktsi/dot_general | solution.py:73
  36.2 13.3 %fusion = f32[128,2048]{1,0:T(8,128)S(1)} fusion(f32[256,8,16,128]{3,2,1,0:T(8,128)} %bitcast.99, s32[2048]{0:T(1024)S(1)} %bitcast.107), kind=kOutput, calls=%fused_computation.3 | convolution fusion | flops 6442713088 | bytes 17833984 | tf_op jit(solution)/shard_map/dot_general | solution.py:44
  49.5 1.2 fusion.10
  50.7 0.0 copy-start.7
  50.7 0.0 copy-start.8
  50.7 1.4 copy.63
  52.1 13.3 %all-to-all-start = ((bf16[64,5,16,128]{3,2,1,0:T(8,128)(2,1)}), bf16[64,5,16,128]{3,2,1,0:T(8,128)(2,1)}, u32[]{:S(2)}, u32[]{:S(2)}) async-start(bf16[64,5,16,128]{3,2,1,0:T(8,128)(2,1)} %bitcast.103), calls=%async_computation | async-start | bytes 2621440 | tf_op jit(solution)/shard_map/all_to_all | solution.py:95
  65.4 0.1 copy.43
  65.5 0.1 eq.121
  65.7 33.3 %all-to-all-done = bf16[64,5,16,128]{3,2,1,0:T(8,128)(2,1)} async-done(((bf16[64,5,16,128]{3,2,1,0:T(8,128)(2,1)}), bf16[64,5,16,128]{3,2,1,0:T(8,128)(2,1)}, u32[]{:S(2)}, u32[]{:S(2)}) %all-to-all-start) | async-done | bytes 1310752 | tf_op jit(solution)/shard_map/all_to_all | solution.py:95
  99.0 1.6 fusion.23
  100.6 0.5 fusion.9
  101.2 0.0 copy-start.2
  101.2 1.4 copy.65
  102.6 6.5 %all-to-all-start.1 = ((bf16[64,5,16,128]{3,2,1,0:T(8,128)(2,1)}), bf16[64,5,16,128]{3,2,1,0:T(8,128)(2,1)}, u32[]{:S(2)}, u32[]{:S(2)}) async-start(bf16[64,5,16,128]{3,2,1,0:T(8,128)(2,1)} %bitcast.102), calls=%async_computation.1 | async-start | bytes 2621440 | tf_op jit(solution)/shard_map/all_to_all | solution.py:103
  109.1 0.2 copy.55
  109.3 3.1 %collective-permute-start = (f32[64,1,128]{2,0,1:T(8,128)S(1)}, f32[64,1,128]{2,0,1:T(8,128)S(1)}, u32[]{:S(2)}, u32[]{:S(2)}) collective-permute-start(f32[64,1,128]{2,0,1:T(8,128)S(1)} %get-tuple-element.10), channel_id=1, source_target_pairs={{0,64},{64,128},{128,192},{1,65},{65,129},{129,193},{2,66},{66,130... | collective-permute-start | bytes 98312 | tf_op jit(solution)/shard_map/ppermute | solution.py:23
  112.4 1.3 collective-permute-start.1
  113.7 0.1 convert_reduce_fusion
  113.8 1.2 gather_fusion
  115.1 0.6 copy.57
  115.7 26.9 %all-to-all-done.1 = bf16[64,5,16,128]{3,2,1,0:T(8,128)(2,1)} async-done(((bf16[64,5,16,128]{3,2,1,0:T(8,128)(2,1)}), bf16[64,5,16,128]{3,2,1,0:T(8,128)(2,1)}, u32[]{:S(2)}, u32[]{:S(2)}) %all-to-all-start.1) | async-done | bytes 1310752 | tf_op jit(solution)/shard_map/all_to_all | solution.py:103
  142.6 6.4 %convert_bitcast_fusion = bf16[256,8,16,128]{3,1,2,0:T(8,128)(2,1)} fusion(bf16[40,8,16,128]{3,2,1,0:T(8,128)(2,1)} %bitcast.36, s32[2048]{0:T(1024)S(1)} %bitcast.108, s32[128]{0:T(128)S(1)} %subtract_add_fusion), kind=kOutput, calls=%fused_computation.10 | convolution fusion | flops 1246273536 | bytes 9708032 | tf_op jit(solution)/shard_map/dot_general | solution.py:37
  149.1 9.8 %copy.67 = bf16[256,8,16,128]{3,2,1,0:T(8,128)(2,1)} copy(bf16[256,8,16,128]{3,1,2,0:T(8,128)(2,1)} %convert_bitcast_fusion) | data formatting | bytes 16777216
  158.8 11.5 %fusion.3 = f32[64,32,16,128]{3,2,1,0:T(8,128)} fusion(bf16[64,128,128]{2,1,0:T(8,128)(2,1)S(1)} %bitcast_select_fusion, bf16[64,32,16,128]{3,2,1,0:T(8,128)(2,1)} %bitcast.101), kind=kOutput, calls=%fused_computation.6 | convolution fusion | flops 1073741824 | bytes 27262976 | tf_op jit(solution)/shard_map/kij,ktsi->ktsj/dot_general | solution.py:111
  170.3 15.7 %copy.98 = f32[256,8,16,128]{3,1,2,0:T(8,128)} copy(f32[256,8,16,128]{3,2,1,0:T(8,128)} %bitcast.98) | data formatting | bytes 33554432
  186.0 17.6 %copy.47 = f32[2048,2048]{1,0:T(8,128)} copy(f32[2048,2048]{0,1:T(8,128)} %bitcast.97) | data formatting | bytes 33554432 | tf_op jit(solution)/shard_map/dot_general | solution.py:44
  203.6 0.0 collective-permute-done
  203.7 0.0 copy-start.1
  203.7 12.8 %fusion.17 = f32[64,16,128]{2,0,1:T(8,128)S(1)} fusion(f32[64,16,128]{2,0,1:T(8,128)S(1)} %copy.55, f32[16,128,2048]{2,1,0:T(8,128)} %bitcast.96, f32[64,1,128]{2,0,1:T(8,128)S(1)} %collective-permute-done.1, f32[64,1,128]{2,0,1:T(8,128)S(1)} %collective-permute-done, f32[64,16,128]{2,1,0:T(8,128)S(1)} %copy-done.3, s32[2048]{0:T(1024)S(1)} %bitcast.106, ...), kind=kOutput, calls=%fused_computation.28 | convolution fusion | flops 3222798336 | bytes 18423840 | tf_op jit(solution)/shard_map/dot_general | solution.py:44
  216.4 1.1 copy.56
  (21 shorter events, 0.1 us)
Async XLA Ops:
  0.6 64.8 %copy-start = (s32[64,64,5]{1,0,2:T(8,128)S(1)}, s32[64,64,5]{1,0,2:T(8,128)}, u32[]{:S(2)}) copy-start(s32[64,64,5]{1,0,2:T(8,128)} %param.17) | copy-start | bytes 245764
  7.9 9.8 %copy-start.6 = (s32[1,64]{1,0:T(1,128)S(1)}, s32[1,64]{1,0:T(1,128)}, u32[]{:S(2)}) copy-start(s32[1,64]{1,0:T(1,128)} %param.16) | copy-start | bytes 772
  24.6 11.5 %copy-start.5 = (s32[1,2048]{1,0:T(1,128)S(1)}, s32[1,2048]{1,0:T(1,128)}, u32[]{:S(2)}) copy-start(s32[1,2048]{1,0:T(1,128)} %param.15) | copy-start | bytes 24580
  50.7 48.3 %copy-start.7 = (f32[6,16,128]{2,1,0:T(8,128)S(1)}, f32[6,16,128]{2,1,0:T(8,128)}, u32[]{:S(2)}) copy-start(f32[6,16,128]{2,1,0:T(8,128)} %param.19) | copy-start | bytes 147460
  50.7 48.3 %copy-start.8 = (f32[6,16,128]{2,1,0:T(8,128)S(1)}, f32[6,16,128]{2,1,0:T(8,128)}, u32[]{:S(2)}) copy-start(f32[6,16,128]{2,1,0:T(8,128)} %param.18) | copy-start | bytes 147460
  52.1 46.9 %all-to-all-start = ((bf16[64,5,16,128]{3,2,1,0:T(8,128)(2,1)}), bf16[64,5,16,128]{3,2,1,0:T(8,128)(2,1)}, u32[]{:S(2)}, u32[]{:S(2)}) async-start(bf16[64,5,16,128]{3,2,1,0:T(8,128)(2,1)} %bitcast.103), calls=%async_computation | async-start | bytes 2621440 | tf_op jit(solution)/shard_map/all_to_all | solution.py:95
  101.2 7.9 %copy-start.2 = (f32[64,16,128]{2,1,0:T(8,128)S(1)}, f32[64,16,128]{2,1,0:T(8,128)}, u32[]{:S(2)}) copy-start(f32[64,16,128]{2,1,0:T(8,128)} %param.10) | copy-start | bytes 1572868
  102.6 40.1 %all-to-all-start.1 = ((bf16[64,5,16,128]{3,2,1,0:T(8,128)(2,1)}), bf16[64,5,16,128]{3,2,1,0:T(8,128)(2,1)}, u32[]{:S(2)}, u32[]{:S(2)}) async-start(bf16[64,5,16,128]{3,2,1,0:T(8,128)(2,1)} %bitcast.102), calls=%async_computation.1 | async-start | bytes 2621440 | tf_op jit(solution)/shard_map/all_to_all | solution.py:103
  109.3 94.4 %collective-permute-start = (f32[64,1,128]{2,0,1:T(8,128)S(1)}, f32[64,1,128]{2,0,1:T(8,128)S(1)}, u32[]{:S(2)}, u32[]{:S(2)}) collective-permute-start(f32[64,1,128]{2,0,1:T(8,128)S(1)} %get-tuple-element.10), channel_id=1, source_target_pairs={{0,64},{64,128},{128,192},{1,65},{65,129},{129,193},{2,66},{66,130... | collective-permute-start | bytes 98312 | tf_op jit(solution)/shard_map/ppermute | solution.py:23
  112.4 91.3 %collective-permute-start.1 = (f32[64,1,128]{2,0,1:T(8,128)S(1)}, f32[64,1,128]{2,0,1:T(8,128)S(1)}, u32[]{:S(2)}, u32[]{:S(2)}) collective-permute-start(f32[64,1,128]{2,0,1:T(8,128)S(1)} %get-tuple-element.11), channel_id=1, source_target_pairs={{64,0},{128,64},{192,128},{65,1},{129,65},{193,129},{66,2},{130,66... | collective-permute-start | bytes 98312 | tf_op jit(solution)/shard_map/ppermute | solution.py:25
  186.0 17.7 %copy-start.3 = (f32[64,16,128]{2,1,0:T(8,128)S(1)}, f32[64,16,128]{2,1,0:T(8,128)}, u32[]{:S(2)}) copy-start(f32[64,16,128]{2,1,0:T(8,128)} %param.11) | copy-start | bytes 1572868
  186.0 17.7 %copy-start.4 = (s32[1,2048]{1,0:T(1,128)S(1)}, s32[1,2048]{1,0:T(1,128)}, u32[]{:S(2)}) copy-start(s32[1,2048]{1,0:T(1,128)} %param.14) | copy-start | bytes 24580
  203.7 13.9 %copy-start.1 = (s32[64,64,5]{1,0,2:T(8,128)S(1)}, s32[64,64,5]{1,0,2:T(8,128)}, u32[]{:S(2)}) copy-start(s32[64,64,5]{1,0,2:T(8,128)} %param.17) | copy-start | bytes 245764
where the time goes:
time: 218 us
  matrix products  64.2 us (29%)
  local copies, waits for them, and re-layouts  64 us (29%)
  waiting for transfers between devices  60.2 us (28%)
  starting transfers between devices  24.2 us (11%)
  other arithmetic  4.1 us (2%)
    unnamed x26, local copies, waits for them, and re-layouts  39.9 us
    all_to_all x1, waiting for transfers between devices, per_device(): lax.all_to_all(outgoing.astype(jnp.bfloat16), 'region', split_axis=0, con...  33.3 us
    dot_general x3, matrix products, sum_rows(): jnp.dot(selector, flat, preferred_element_type=jnp.float32, precision=lax...  27.7 us
    all_to_all x1, waiting for transfers between devices, per_device(): lax.all_to_all(returning, 'region', split_axis=0, concat_axis=0, tiled=True)  26.9 us
    dot_general x1, local copies, waits for them, and re-layouts, sum_rows(): jnp.dot(selector, flat, preferred_element_type=jnp.float32, precision=lax...  17.6 us
    all_to_all x1, starting transfers between devices, per_device(): lax.all_to_all(outgoing.astype(jnp.bfloat16), 'region', split_axis=0, con...  13.3 us
    dot_general x3, matrix products, pick_rows(): jnp.dot(selector, flat, preferred_element_type=jnp.float32)  12.3 us
    dot_general x1, matrix products, per_device(): jnp.einsum('kij,ktsj->ktsi', footprints, gathered, preferred_element_type...  11.5 us
  transfers between devices with their start and end apart: 4, of which 2 were waited for; matrix products, arithmetic and copies ran while one was open for 29% of the time, Pallas kernels for 0%

commit v1 on v0

v1 whole, which is shorter than its diff:
```python
import functools

import jax
import jax.numpy as jnp
from jax import lax
from jax.experimental import pallas as pl
from jax.experimental.pallas import tpu as pltpu
from jax.sharding import PartitionSpec as P

ANG = 16
SHIFTS = 4
OWN = 6
CAP = 5
NZ, NY, NC = 8, 4, 2
smoothing_weight = 0.5
NACC = 4


def fill_rays(counts, owner_map, place, rays):
    def owner(d, start):
        base = place[d]
        for p in range(CAP):
            rays[start + p] = base + owner_map[d * CAP + p]
        return start + counts[d]

    lax.fori_loop(0, NZ * NY * NC, owner, jnp.int32(0))


def forward_kernel(subset, pixels, slots, counts, owner_map, place, table, image, out, xb, rays, *accs):
    step = pl.program_id(0)
    tiles = pixels.shape[0] // (ANG * SHIFTS)

    @pl.when(step == 0)
    def _():
        fill_rays(counts, owner_map, place, rays)
        xb[...] = image[...].astype(jnp.bfloat16)
        for acc in accs:
            acc[...] = jnp.zeros_like(acc)

    slabs = xb.shape[1]
    for shift in range(SHIFTS):
        base = (step * SHIFTS + shift) * tiles
        x = jnp.concatenate([xb[pixels[base + t]] for t in range(tiles)], axis=0)
        y = lax.dot_general(
            x, table[0, shift], (((1,), (1,)), ((), ())), preferred_element_type=jnp.float32
        )
        for t in range(tiles):
            acc = accs[t % len(accs)]
            row = rays[slots[base + t]]
            acc[row] += y[t * slabs : (t + 1) * slabs]

    @pl.when(step == ANG - 1)
    def _():
        @pl.loop(0, out.shape[0], unroll=4)
        def _(r):
            out[r] = sum(acc[r] for acc in accs).astype(jnp.bfloat16)


def backward_kernel(subset, pixels, slots, counts, owner_map, place, table, mine, theirs, start, precond, out, rb, rays, *accs):
    step = pl.program_id(0)
    tiles = pixels.shape[0] // (ANG * SHIFTS)

    @pl.when(step == 0)
    def _():
        fill_rays(counts, owner_map, place, rays)
        half = mine.shape[0]
        rb[:half] = mine[...]
        rb[half:] = theirs[...]
        for acc in accs:
            acc[...] = jnp.zeros_like(acc)

    slabs = rb.shape[1]
    for shift in range(SHIFTS):
        base = (step * SHIFTS + shift) * tiles
        x = jnp.concatenate([rb[rays[slots[base + t]]] for t in range(tiles)], axis=0)
        y = jnp.dot(x, table[0, shift], preferred_element_type=jnp.float32)
        for t in range(tiles):
            acc = accs[t % len(accs)]
            row = pixels[base + t]
            acc[row] += y[t * slabs : (t + 1) * slabs]

    @pl.when(step == ANG - 1)
    def _():
        @pl.loop(0, out.shape[0], unroll=4)
        def _(r):
            out[r] = start[r] + sum(acc[r] for acc in accs) / precond[r]


def whole(array):
    return pl.BlockSpec(array.shape, lambda a, *_: (0,) * array.ndim)


def table_spec(table):
    return pl.BlockSpec((1,) + table.shape[1:], lambda a, subset, *_: (subset[a], 0, 0, 0))


def call(kernel, name, scalars, table, dense, out, width, rows, flops, bytes_moved):
    slabs, lanes = dense[0].shape[1:]
    return pl.pallas_call(
        kernel,
        name=name,
        out_shape=out,
        grid_spec=pltpu.PrefetchScalarGridSpec(
            num_scalar_prefetch=len(scalars),
            grid=(ANG,),
            in_specs=[table_spec(table)] + [whole(d) for d in dense],
            out_specs=whole(out),
            scratch_shapes=[
                pltpu.VMEM((width, slabs, lanes), jnp.bfloat16),
                pltpu.SMEM((160,), jnp.int32),
            ]
            + [pltpu.VMEM((rows, slabs, lanes), jnp.float32)] * NACC,
        ),
        compiler_params=pltpu.CompilerParams(
            dimension_semantics=("arbitrary",), vmem_limit_bytes=40 << 20
        ),
        cost_estimate=pl.CostEstimate(flops=flops, bytes_accessed=bytes_moved, transcendentals=0),
    )(*scalars, table, *dense)


def index_of(z, y, c):
    return (z * NY + y) * NC + c


GROUP_Y = [[index_of(z, y, c) for y in range(NY)] for z in range(NZ) for c in range(NC)]
GROUP_Z = [[index_of(z, y, c) for z in range(NZ)] for y in range(NY) for c in range(NC)]
SWAP = [(i, i ^ 1) for i in range(NZ * NY * NC)]


def exchange(x, groups):
    return lax.all_to_all(
        x, "region", split_axis=0, concat_axis=0, tiled=True, axis_index_groups=groups
    )


def per_device(
    image, precond, table, subset, tile_pixel, tile_slot, send_count, recv_map, measured, stat_weight
):
    blocks, slabs, lanes = image.shape
    me = lax.axis_index("region")
    core = me % NC
    owners = jnp.arange(NZ * NY * NC, dtype=jnp.int32)
    oz, oy, oc = owners // (NY * NC), owners // NC % NY, owners % NC
    place = (((oc ^ core) * NY + oy) * NZ + oz) * OWN
    owner_map = lax.dynamic_index_in_dim(recv_map, me, 1, keepdims=False).reshape(-1)
    scalars = (subset, tile_pixel[0], tile_slot[0], send_count[0], owner_map, place.astype(jnp.int32))
    rows = NZ * NY * NC * OWN
    half = rows // 2

    cuts = lax.axis_size("cuts")
    up = [(i, i + 1) for i in range(cuts - 1)]
    before = lax.ppermute(image[:, -1:, :], "cuts", up)
    after = lax.ppermute(image[:, :1, :], "cuts", [(j, i) for i, j in up])

    local = call(
        forward_kernel, "project", scalars, table, (image,),
        jax.ShapeDtypeStruct((rows, slabs, lanes), jnp.bfloat16), blocks, rows,
        2 * 2048 * slabs * lanes * lanes, 6 << 20,
    )
    other = lax.ppermute(local[half:], "region", SWAP)
    chip = (local[:half].astype(jnp.float32) + other.astype(jnp.float32)).astype(jnp.bfloat16)
    got = exchange(chip, GROUP_Y).reshape(NY, NZ * OWN, slabs, lanes)
    row = jnp.sum(got.astype(jnp.float32), axis=0).astype(jnp.bfloat16)
    got = exchange(row, GROUP_Z).reshape(NZ, OWN, slabs, lanes)
    summed = jnp.sum(got.astype(jnp.float32), axis=0)
    residual = stat_weight * (measured - summed)
    resid_half = residual.astype(jnp.bfloat16)

    back = exchange(jnp.tile(resid_half, (NZ, 1, 1, 1)).reshape(NZ * OWN, slabs, lanes), GROUP_Z)
    back = lax.all_gather(back, "region", axis=0, tiled=True, axis_index_groups=GROUP_Y)
    theirs = lax.ppermute(back, "region", SWAP)

    padded = jnp.concatenate([before, image, after], axis=1)
    global_slice = lax.axis_index("cuts") * slabs + jnp.arange(slabs, dtype=jnp.int32)
    below = jnp.where((global_slice > 0)[None, :, None], image - padded[:, :-2, :], 0.0)
    above = jnp.where(
        (global_slice < slabs * cuts - 1)[None, :, None], image - padded[:, 2:, :], 0.0
    )
    start = image - smoothing_weight * (below + above) / precond
    updated = call(
        backward_kernel, "backproject", scalars, table, (back, theirs, start, precond),
        jax.ShapeDtypeStruct(image.shape, jnp.float32), rows, blocks,
        2 * 2048 * slabs * lanes * lanes, 6 << 20,
    )
    return (updated, residual)


def solution(mesh):
    in_specs = (
        P("region", "cuts", None),
        P("region", "cuts", None),
        P(),
        P(),
        P("region", None),
        P("region", None),
        P("region", None),
        P(),
        P("region", "cuts", None),
        P("region", "cuts", None),
    )
    out_specs = (P("region", "cuts", None), P("region", "cuts", None))
    return jax.shard_map(
        per_device, mesh=mesh, in_specs=in_specs, out_specs=out_specs, check_vma=False
    )
```

time: 218 us -> 106 us (0.49)
  matrix products: 64.2 us -> 0 us
  waiting for transfers between devices: 60.2 us -> 5.25 us
  local copies, waits for them, and re-layouts: 64 us -> 9.99 us
  blocking collectives: 0 us -> 53 us
  Pallas kernels: 0 us -> 19.7 us
  starting transfers between devices: 24.2 us -> 14.8 us
  other arithmetic: 4.1 us -> 1.33 us
    dot_general x9 -> x0, matrix products: 64.2 us -> none  [the longest x3 27.7 us: sum_rows(): jnp.dot(selector, flat, preferred_element_type=jnp.float32, precision=lax...]
    all_to_all x2 -> x0, waiting for transfers between devices: 60.2 us -> none  [the longest x1 33.3 us: per_device(): lax.all_to_all(outgoing.astype(jnp.bfloat16), 'region', split_axis=0, con...]
    all_to_all x0 -> x3, blocking collectives: none -> 41.9 us  [exchange(): lax.all_to_all(x, 'region', split_axis=0, concat_axis=0, tiled=True, axis...]
    unnamed x26 -> x32, local copies, waits for them, and re-layouts: 39.9 us -> 9.05 us
    all_to_all x2 -> x0, starting transfers between devices: 19.8 us -> none  [the longest x1 13.3 us: per_device(): lax.all_to_all(outgoing.astype(jnp.bfloat16), 'region', split_axis=0, con...]
    pallas_call x0 -> x2, Pallas kernels: none -> 19.7 us  [call(): pl.pallas_call(kernel, name=name, out_shape=out, grid_spec=pltpu.Prefetch...]
    dot_general x1 -> x0, local copies, waits for them, and re-layouts: 17.6 us -> none  [sum_rows(): jnp.dot(selector, flat, preferred_element_type=jnp.float32, precision=lax...]
    all_gather x0 -> x1, blocking collectives: none -> 11.1 us  [per_device(): lax.all_gather(back, 'region', axis=0, tiled=True, axis_index_groups=GROU...]
  transfers between devices with their start and end apart: 4 -> 4, of which waited for: 2 -> 2; matrix products, arithmetic and copies ran while one was open for 29% -> 0% of each run, Pallas kernels for 0% -> 0%
where the time goes in v1:
time: 106 us; the launch traced here: 105 us
  blocking collectives  53 us (50%)
  Pallas kernels  19.7 us (19%)
  starting transfers between devices  14.8 us (14%)
  local copies, waits for them, and re-layouts  9.99 us (9%)
  waiting for transfers between devices  5.25 us (5%)
  other arithmetic  1.33 us (1%)
    all_to_all x3, blocking collectives, exchange(): lax.all_to_all(x, 'region', split_axis=0, concat_axis=0, tiled=True, axis...  41.9 us
    pallas_call x2, Pallas kernels, call(): pl.pallas_call(kernel, name=name, out_shape=out, grid_spec=pltpu.Prefetch...  19.7 us
    all_gather x1, blocking collectives, per_device(): lax.all_gather(back, 'region', axis=0, tiled=True, axis_index_groups=GROU...  11.1 us
    unnamed x32, local copies, waits for them, and re-layouts  9.05 us
    ppermute x1, starting transfers between devices, per_device(): theirs = lax.ppermute(back, 'region', SWAP)  7.12 us
    ppermute x1, waiting for transfers between devices, per_device(): after = lax.ppermute(image[:, :1, :], 'cuts', [(j, i) for i, j in up])  3.33 us
    ppermute x1, starting transfers between devices, per_device(): other = lax.ppermute(local[half:], 'region', SWAP)  3.29 us
    ppermute x1, starting transfers between devices, per_device(): before = lax.ppermute(image[:, -1:, :], 'cuts', up)  3.11 us
  transfers between devices with their start and end apart: 4, of which 2 were waited for; matrix products, arithmetic and copies ran while one was open for 0% of the time, Pallas kernels for 0%

profile of v1, /device:TPU:1, one launch (start us, length us, event | category | flops | bytes accessed | tf_op | source)
XLA Modules:
  0.0 104.9 jit_solution(16738015309268889730)
XLA Ops:
  0.6 0.0 copy-start
  0.7 0.9 copy-done
  1.6 0.1 constant_dynamic-slice_fusion
  1.7 0.5 copy.14
  2.1 0.1 reshape.26.owner_map
  2.3 0.0 copy-start.1
  2.3 2.2 %copy-done.1 = bf16[32,4,128,128]{3,2,1,0:T(8,128)(2,1)S(1)} copy-done((bf16[32,4,128,128]{3,2,1,0:T(8,128)(2,1)S(1)}, bf16[32,4,128,128]{3,2,1,0:T(8,128)(2,1)}, u32[]{:S(2)}) %copy-start.1) | copy-done | bytes 4194328
  4.5 0.0 copy-start.3
  4.5 1.0 copy-done.3
  5.5 0.7 copy-done.6
  6.2 0.7 copy-done.8
  6.9 0.7 copy-done.10
  7.6 0.7 copy-done.12
  8.2 10.3 %project.1 = bf16[384,16,128]{2,1,0:T(8,128)(2,1)S(1)} custom-call(s32[32]{0:T(128)S(1)} %copy-done.10, s32[2048]{0:T(1024)S(1)} %bitcast.9, s32[2048]{0:T(1024)S(1)} %bitcast.11, s32[64]{0:T(128)S(1)} %bitcast.13, s32[320]{0:T(512)S(1)} %reshape.26.owner_map, s32[64]{0:T(128)S(1)} %fusion.10.place, bf16[32,4,128,128]{3,2,1,0:T(8,128)(2,1)S(1)} %copy-done.1, ...), custom_call_target="tpu_custom_call" | custom-call | flops 1073741824 | bytes 6291456 | tf_op jit(solution)/shard_map/project/pallas_call | solution.py:99
  18.5 0.1 slice.27
  18.7 3.3 %collective-permute-start = (bf16[192,16,128]{2,1,0:T(8,128)(2,1)S(1)}, bf16[192,16,128]{2,1,0:T(8,128)(2,1)S(1)}, u32[]{:S(2)}, u32[]{:S(2)}) collective-permute-start(bf16[192,16,128]{2,1,0:T(8,128)(2,1)S(1)} %slice.27), channel_id=1, source_target_pairs={{0,1},{1,0},{2,3},{3,2},{4,5},{5,4},{6,7},{7,6},{8,9},{9,8},{10,11... | collective-permute-start | bytes 2359304 | tf_op jit(solution)/shard_map/ppermute | solution.py:160
  21.9 1.9 %collective-permute-done = bf16[192,16,128]{2,1,0:T(8,128)(2,1)S(1)} collective-permute-done((bf16[192,16,128]{2,1,0:T(8,128)(2,1)S(1)}, bf16[192,16,128]{2,1,0:T(8,128)(2,1)S(1)}, u32[]{:S(2)}, u32[]{:S(2)}) %collective-permute-start) | collective-permute-done | bytes 786464 | tf_op jit(solution)/shard_map/ppermute | solution.py:160
  23.9 0.2 add_convert_fusion
  24.1 0.0 copy-start.14
  24.1 0.0 copy-start.15
  24.1 14.4 %all_to_all.15 = bf16[192,16,128]{2,1,0:T(8,128)(2,1)S(1)} all-to-all(bf16[192,16,128]{2,1,0:T(8,128)(2,1)S(1)} %add_convert_fusion), channel_id=1, replica_groups={{0,2,4,6},{1,3,5,7},{8,10,12,14},{9,11,13,15},{16,18,20,22},{17,19,21,2..., dimensions={0} | all-to-all | bytes 1572864 | tf_op jit(solution)/shard_map/all_to_all | solution.py:131
  38.5 0.2 reduce_sum.21
  38.7 16.2 %all_to_all.16 = bf16[48,16,128]{2,1,0:T(8,128)(2,1)S(1)} all-to-all(bf16[48,16,128]{2,1,0:T(8,128)(2,1)S(1)} %reduce_sum.21), channel_id=1, replica_groups={{0,8,16,24,32,40,48,56},{1,9,17,25,33,41,49,57},{2,10,18,26,34,42,50,58..., dimensions={0} | all-to-all | bytes 393216 | tf_op jit(solution)/shard_map/all_to_all | solution.py:131
  54.9 0.0 copy-done.14
  54.9 0.0 copy-done.15
  55.0 0.6 fusion.17
  55.6 0.0 copy-start.7
  55.6 0.0 copy-start.9
  55.6 0.0 copy-start.11
  55.7 0.0 copy-start.13
  55.7 11.3 %all_to_all.17 = bf16[48,16,128]{2,1,0:T(8,128)(2,1)S(1)} all-to-all(bf16[48,16,128]{2,1,0:T(8,128)(2,1)S(1)} %bitcast.16), channel_id=1, replica_groups={{0,8,16,24,32,40,48,56},{1,9,17,25,33,41,49,57},{2,10,18,26,34,42,50,58..., dimensions={0} | all-to-all | bytes 393216 | tf_op jit(solution)/shard_map/all_to_all | solution.py:131
  66.9 11.1 %all_gather.3.mine = bf16[192,16,128]{2,1,0:T(8,128)(2,1)S(1)} all-gather(bf16[48,16,128]{2,1,0:T(8,128)(2,1)S(1)} %all_to_all.17), channel_id=1, replica_groups={{0,2,4,6},{1,3,5,7},{8,10,12,14},{9,11,13,15},{16,18,20,22},{17,19,21,2..., dimensions={0}, use_global_device_ids=true | all-gather | bytes 983040 | tf_op jit(solution)/shard_map/all_gather | solution.py:170
  78.0 7.1 %collective-permute-start.1 = (bf16[192,16,128]{2,1,0:T(8,128)(2,1)S(1)}, bf16[192,16,128]{2,1,0:T(8,128)(2,1)S(1)}, u32[]{:S(2)}, u32[]{:S(2)}) collective-permute-start(bf16[192,16,128]{2,1,0:T(8,128)(2,1)S(1)} %all_gather.3.mine), channel_id=1, source_target_pairs={{0,1},{1,0},{2,3},{3,2},{4,5},{5,4},{6,7},{7,6},{8,9},{9,8},{10,11... | collective-permute-start | bytes 2359304 | tf_op jit(solution)/shard_map/ppermute | solution.py:171
  85.1 0.0 copy-done.4
  85.1 3.1 %collective-permute-start.2 = (f32[64,1,128]{2,1,0:T(1,128)S(1)}, f32[64,1,128]{2,1,0:T(1,128)S(1)}, u32[]{:S(2)}, u32[]{:S(2)}) collective-permute-start(f32[64,1,128]{2,1,0:T(1,128)S(1)} %get-tuple-element.4), channel_id=1, source_target_pairs={{0,64},{64,128},{128,192},{1,65},{65,129},{129,193},{2,66},{66,130... | collective-permute-start | bytes 98312 | tf_op jit(solution)/shard_map/ppermute | solution.py:152
  88.3 1.3 %collective-permute-start.3 = (f32[64,1,128]{2,1,0:T(1,128)S(1)}, f32[64,1,128]{2,1,0:T(1,128)S(1)}, u32[]{:S(2)}, u32[]{:S(2)}) collective-permute-start(f32[64,1,128]{2,1,0:T(1,128)S(1)} %get-tuple-element.5), channel_id=1, source_target_pairs={{64,0},{128,64},{192,128},{65,1},{129,65},{193,129},{66,2},{130,66... | collective-permute-start | bytes 98312 | tf_op jit(solution)/shard_map/ppermute | solution.py:153
  89.6 0.0 collective-permute-done.2
  89.6 3.3 %collective-permute-done.3 = f32[64,1,128]{2,1,0:T(1,128)S(1)} collective-permute-done((f32[64,1,128]{2,1,0:T(1,128)S(1)}, f32[64,1,128]{2,1,0:T(1,128)S(1)}, u32[]{:S(2)}, u32[]{:S(2)}) %collective-permute-start.3) | collective-permute-done | bytes 32800 | tf_op jit(solution)/shard_map/ppermute | solution.py:153
  92.9 0.0 copy-done.5
  92.9 0.3 fusion.5.start
  93.2 0.0 collective-permute-done.1.theirs
  93.2 0.0 copy-done.7
  93.2 0.0 copy-done.9
  93.2 0.0 copy-done.11
  93.3 0.0 copy-done.13
  93.3 0.0 copy-start.2
  93.3 2.2 %copy-done.2 = bf16[32,4,128,128]{3,2,1,0:T(8,128)(2,1)S(1)} copy-done((bf16[32,4,128,128]{3,2,1,0:T(8,128)(2,1)S(1)}, bf16[32,4,128,128]{3,2,1,0:T(8,128)(2,1)}, u32[]{:S(2)}) %copy-start.2) | copy-done | bytes 4194328
  95.5 9.5 %backproject.1 = f32[64,16,128]{2,1,0:T(8,128)} custom-call(s32[32]{0:T(128)S(1)} %copy-done.11, s32[2048]{0:T(1024)S(1)} %bitcast.10, s32[2048]{0:T(1024)S(1)} %bitcast.12, s32[64]{0:T(128)S(1)} %bitcast.14, s32[320]{0:T(512)S(1)} %reshape.26.owner_map, s32[64]{0:T(128)S(1)} %fusion.10.place, bf16[32,4,128,128]{3,2,1,0:T(8,128)(2,1)S(1)} %copy-done.2, ...), custom_call_target="tpu_custom_call" | custom-call | flops 1073741824 | bytes 6291456 | tf_op jit(solution)/shard_map/backproject/pallas_call | solution.py:99
  (11 shorter events, 0.1 us)
Async XLA Ops:
  0.6 0.9 copy-start
  2.3 2.2 %copy-start.1 = (bf16[32,4,128,128]{3,2,1,0:T(8,128)(2,1)S(1)}, bf16[32,4,128,128]{3,2,1,0:T(8,128)(2,1)}, u32[]{:S(2)}) copy-start(bf16[32,4,128,128]{3,2,1,0:T(8,128)(2,1)} %table.3) | copy-start | bytes 12582916
  4.5 1.0 copy-start.3
  5.5 0.7 copy-start.6
  6.2 0.7 copy-start.8
  6.9 0.7 copy-start.10
  7.6 0.7 copy-start.12
  18.7 5.2 %collective-permute-start = (bf16[192,16,128]{2,1,0:T(8,128)(2,1)S(1)}, bf16[192,16,128]{2,1,0:T(8,128)(2,1)S(1)}, u32[]{:S(2)}, u32[]{:S(2)}) collective-permute-start(bf16[192,16,128]{2,1,0:T(8,128)(2,1)S(1)} %slice.27), channel_id=1, source_target_pairs={{0,1},{1,0},{2,3},{3,2},{4,5},{5,4},{6,7},{7,6},{8,9},{9,8},{10,11... | collective-permute-start | bytes 2359304 | tf_op jit(solution)/shard_map/ppermute | solution.py:160
  24.1 30.9 %copy-start.14 = (f32[6,16,128]{2,1,0:T(8,128)S(1)}, f32[6,16,128]{2,1,0:T(8,128)}, u32[]{:S(2)}) copy-start(f32[6,16,128]{2,1,0:T(8,128)} %param.19) | copy-start | bytes 147460
  24.1 30.9 %copy-start.15 = (f32[6,16,128]{2,1,0:T(8,128)S(1)}, f32[6,16,128]{2,1,0:T(8,128)}, u32[]{:S(2)}) copy-start(f32[6,16,128]{2,1,0:T(8,128)} %param.18) | copy-start | bytes 147460
  38.5 46.6 %copy-start.4 = (f32[64,16,128]{2,1,0:T(8,128)S(1)}, f32[64,16,128]{2,1,0:T(8,128)}, u32[]{:S(2)}) copy-start(f32[64,16,128]{2,1,0:T(8,128)} %image.1) | copy-start | bytes 1572868
  38.5 54.4 %copy-start.5 = (f32[64,16,128]{2,1,0:T(8,128)S(1)}, f32[64,16,128]{2,1,0:T(8,128)}, u32[]{:S(2)}) copy-start(f32[64,16,128]{2,1,0:T(8,128)} %precond.1) | copy-start | bytes 1572868
  55.6 37.6 %copy-start.7 = (s32[1,2048]{1,0:T(1,128)S(1)}, s32[1,2048]{1,0:T(1,128)}, u32[]{:S(2)}) copy-start(s32[1,2048]{1,0:T(1,128)} %param.14) | copy-start | bytes 24580
  55.6 37.6 %copy-start.9 = (s32[1,2048]{1,0:T(1,128)S(1)}, s32[1,2048]{1,0:T(1,128)}, u32[]{:S(2)}) copy-start(s32[1,2048]{1,0:T(1,128)} %param.15) | copy-start | bytes 24580
  55.6 37.6 %copy-start.11 = (s32[32]{0:T(128)S(1)}, s32[32]{0:T(128)}, u32[]{:S(2)}) copy-start(s32[32]{0:T(128)} %subset.3) | copy-start | bytes 388
  55.7 37.6 %copy-start.13 = (s32[1,64]{1,0:T(1,128)S(1)}, s32[1,64]{1,0:T(1,128)}, u32[]{:S(2)}) copy-start(s32[1,64]{1,0:T(1,128)} %param.16) | copy-start | bytes 772
  78.0 15.2 %collective-permute-start.1 = (bf16[192,16,128]{2,1,0:T(8,128)(2,1)S(1)}, bf16[192,16,128]{2,1,0:T(8,128)(2,1)S(1)}, u32[]{:S(2)}, u32[]{:S(2)}) collective-permute-start(bf16[192,16,128]{2,1,0:T(8,128)(2,1)S(1)} %all_gather.3.mine), channel_id=1, source_target_pairs={{0,1},{1,0},{2,3},{3,2},{4,5},{5,4},{6,7},{7,6},{8,9},{9,8},{10,11... | collective-permute-start | bytes 2359304 | tf_op jit(solution)/shard_map/ppermute | solution.py:171
  85.1 4.4 %collective-permute-start.2 = (f32[64,1,128]{2,1,0:T(1,128)S(1)}, f32[64,1,128]{2,1,0:T(1,128)S(1)}, u32[]{:S(2)}, u32[]{:S(2)}) collective-permute-start(f32[64,1,128]{2,1,0:T(1,128)S(1)} %get-tuple-element.4), channel_id=1, source_target_pairs={{0,64},{64,128},{128,192},{1,65},{65,129},{129,193},{2,66},{66,130... | collective-permute-start | bytes 98312 | tf_op jit(solution)/shard_map/ppermute | solution.py:152
  88.3 4.7 %collective-permute-start.3 = (f32[64,1,128]{2,1,0:T(1,128)S(1)}, f32[64,1,128]{2,1,0:T(1,128)S(1)}, u32[]{:S(2)}, u32[]{:S(2)}) collective-permute-start(f32[64,1,128]{2,1,0:T(1,128)S(1)} %get-tuple-element.5), channel_id=1, source_target_pairs={{64,0},{128,64},{192,128},{65,1},{129,65},{193,129},{66,2},{130,66... | collective-permute-start | bytes 98312 | tf_op jit(solution)/shard_map/ppermute | solution.py:153
  93.3 2.2 %copy-start.2 = (bf16[32,4,128,128]{3,2,1,0:T(8,128)(2,1)S(1)}, bf16[32,4,128,128]{3,2,1,0:T(8,128)(2,1)}, u32[]{:S(2)}) copy-start(bf16[32,4,128,128]{3,2,1,0:T(8,128)(2,1)} %table.3) | copy-start | bytes 12582916

commit v2 on v1

v2 whole, which is shorter than its diff:
```python
import jax
import jax.numpy as jnp
from jax import lax
from jax.experimental import pallas as pl
from jax.experimental.pallas import tpu as pltpu
from jax.sharding import PartitionSpec as P

ANG = 16
SHIFTS = 4
OWN = 6
CAP = 5
NZ, NY, NC = 8, 4, 2
smoothing_weight = 0.5
NACC = 4
WINDOWS = 4
VMEM = 48 << 20
LOC = 128
SLABS = 16
LANES = 128


def fill_rays(counts, owner_rows, rays):
    def owner(d, start):
        for p in range(CAP):
            rays[start + p] = owner_rows[p, d]
        return start + counts[0, d]

    lax.fori_loop(0, NZ * NY * NC, owner, jnp.int32(0))


class Tables:
    def __init__(self, pixels, slots, counts, owner_rows, subset, table, scratch):
        (self.counts_s, self.owner_s, self.subset_s, self.rays, self.table_v,
         self.sems, self.table_sems, self.window_sems) = scratch[:8]
        self.windows = [scratch[8 + 2 * b : 10 + 2 * b] for b in range(WINDOWS)]
        self.pixels, self.slots, self.table = pixels, slots, table
        self.small = [
            pltpu.make_async_copy(source, target, self.sems.at[i])
            for i, (source, target) in enumerate(
                ((subset, self.subset_s), (counts, self.counts_s), (owner_rows, self.owner_s))
            )
        ]

    def window(self, a, b):
        here = pl.ds(pl.multiple_of(a * LANES, LANES), LANES)
        return [
            pltpu.make_async_copy(source.at[:, here], target, self.window_sems.at[i, b])
            for i, (source, target) in enumerate(zip((self.pixels, self.slots), self.windows[b]))
        ]

    def footprints(self, row, a):
        return pltpu.make_async_copy(self.table.at[row], self.table_v.at[a], self.table_sems.at[a])

    def start(self, cleared):
        for copy in self.small:
            copy.start()
        for b in range(WINDOWS):
            for copy in self.window(b, b):
                copy.start()
        for ref in cleared:
            ref[...] = jnp.zeros_like(ref)
        self.small[0].wait()
        for a in range(ANG):
            self.footprints(self.subset_s[a], a).start()
        self.small[1].wait()
        self.small[2].wait()
        fill_rays(self.counts_s, self.owner_s, self.rays)

    def sweep(self, source, accs, take_slot, contract):
        tiles = LANES // SHIFTS

        @pl.loop(0, ANG // WINDOWS)
        def _(g):
            for b in range(WINDOWS):
                a = g * WINDOWS + b
                for copy in self.window(a, b):
                    copy.wait()
                self.footprints(0, a).wait()
                pixel, slot = self.windows[b]
                take, put = (slot, pixel) if take_slot else (pixel, slot)
                for shift in range(SHIFTS):
                    base = shift * tiles
                    x = jnp.concatenate([source[take[0, base + t]] for t in range(tiles)], axis=0)
                    y = lax.dot_general(
                        x, self.table_v[a, shift], (((1,), (contract,)), ((), ())),
                        preferred_element_type=jnp.float32,
                    )
                    for t in range(tiles):
                        acc = accs[t % NACC]
                        acc[put[0, base + t]] += y[t * SLABS : (t + 1) * SLABS]

                @pl.when(g < ANG // WINDOWS - 1)
                def _():
                    for copy in self.window(a + WINDOWS, b):
                        copy.start()


def forward_kernel(pixels, slots, counts, owner_rows, subset, table, image, mine, theirs, low, high, *scratch):
    image_v, xb, total, image_sem = scratch[:4]
    accs = scratch[4 : 4 + NACC]
    tables = Tables(pixels, slots, counts, owner_rows, subset, table, scratch[4 + NACC :])
    image_copy = pltpu.make_async_copy(image, image_v, image_sem)
    image_copy.start()
    tables.start((*accs, total))
    image_copy.wait()
    xb[...] = image_v[...].astype(jnp.bfloat16)
    low[...] = image_v[:, :1, :]
    high[...] = image_v[:, SLABS - 1 :, :]
    tables.sweep(xb, accs, False, 1)

    @pl.loop(0, LOC, unroll=8)
    def _(j):
        total[tables.rays[j]] += sum(acc[j] for acc in accs)

    half = mine.shape[0]
    mine[...] = total[:half].astype(jnp.bfloat16)
    theirs[...] = total[half:].astype(jnp.bfloat16)


def backward_kernel(pixels, slots, counts, owner_rows, subset, table, mine, theirs, start, precond, out, *scratch):
    rb, slot_resid = scratch[:2]
    accs = scratch[2 : 2 + NACC]
    tables = Tables(pixels, slots, counts, owner_rows, subset, table, scratch[2 + NACC :])
    tables.start(accs)
    half = mine.shape[0]
    rb[:half] = mine[...]
    rb[half:] = theirs[...]

    @pl.loop(0, LOC, unroll=8)
    def _(j):
        slot_resid[j] = rb[tables.rays[j]]

    tables.sweep(slot_resid, accs, True, 0)
    out[...] = start[...] + sum(acc[...] for acc in accs) / precond[...]


VM = pl.BlockSpec(memory_space=pltpu.VMEM)
ANYWHERE = pl.BlockSpec(memory_space=pltpu.HBM)


def call(kernel, name, operands, specs, out, dense, acc_rows, flops, bytes_moved):
    table = operands[5]
    several = isinstance(out, (tuple, list))
    return pl.pallas_call(
        kernel,
        name=name,
        out_shape=out,
        in_specs=[ANYWHERE] * 6 + specs,
        out_specs=[VM] * len(out) if several else VM,
        scratch_shapes=dense
        + [pltpu.VMEM((acc_rows, SLABS, LANES), jnp.float32)] * NACC
        + [pltpu.SMEM(operand.shape, jnp.int32) for operand in operands[2:5]]
        + [
            pltpu.SMEM((160,), jnp.int32),
            pltpu.VMEM((ANG,) + table.shape[1:], table.dtype),
            pltpu.SemaphoreType.DMA((3,)),
            pltpu.SemaphoreType.DMA((ANG,)),
            pltpu.SemaphoreType.DMA((2, WINDOWS)),
        ]
        + [pltpu.SMEM((1, LANES), jnp.int32)] * (2 * WINDOWS),
        compiler_params=pltpu.CompilerParams(vmem_limit_bytes=VMEM),
        cost_estimate=pl.CostEstimate(flops=flops, bytes_accessed=bytes_moved, transcendentals=0),
    )(*[
        pltpu.with_memory_space_constraint(operand, pltpu.HBM) if pinned else operand
        for operand, pinned in zip(operands, [i != 3 for i in range(6)] + [s is ANYWHERE for s in specs])
    ])


def index_of(z, y, c):
    return (z * NY + y) * NC + c


GROUP_Y = [[index_of(z, y, c) for y in range(NY)] for z in range(NZ) for c in range(NC)]
GROUP_Z = [[index_of(z, y, c) for z in range(NZ)] for y in range(NY) for c in range(NC)]
SWAP = [(i, i ^ 1) for i in range(NZ * NY * NC)]


def exchange(x, groups):
    return lax.all_to_all(
        x, "region", split_axis=0, concat_axis=0, tiled=True, axis_index_groups=groups
    )


def per_device(
    image, precond, table, subset, tile_pixel, tile_slot, send_count, recv_map, measured, stat_weight
):
    blocks, slabs, lanes = image.shape
    me = lax.axis_index("region")
    core = me % NC
    owners = jnp.arange(NZ * NY * NC, dtype=jnp.int32)
    oz, oy, oc = owners // (NY * NC), owners // NC % NY, owners % NC
    place = (((oc ^ core) * NY + oy) * NZ + oz) * OWN
    mine = jnp.arange(NZ * NY * NC, dtype=jnp.int32) == me
    owner_rows = place[None, :] + jnp.sum(
        jnp.where(mine[None, None, :], recv_map.transpose(2, 0, 1), 0), axis=2
    )
    tables = (tile_pixel, tile_slot, send_count, owner_rows.astype(jnp.int32), subset, table)
    rows = NZ * NY * NC * OWN
    half = rows // 2

    local = jax.ShapeDtypeStruct((half, slabs, lanes), jnp.bfloat16)
    edge = jax.ShapeDtypeStruct((blocks, 1, lanes), jnp.float32)
    kept, given, low, high = call(
        forward_kernel, "project", tables + (image,), [ANYWHERE], (local, local, edge, edge),
        [
            pltpu.VMEM((blocks, slabs, lanes), jnp.float32),
            pltpu.VMEM((blocks, slabs, lanes), jnp.bfloat16),
            pltpu.VMEM((rows, slabs, lanes), jnp.float32),
            pltpu.SemaphoreType.DMA,
        ],
        LOC, 2 * 2048 * slabs * lanes * lanes, 6 << 20,
    )
    cuts = lax.axis_size("cuts")
    up = [(i, i + 1) for i in range(cuts - 1)]
    other = lax.ppermute(given, "region", SWAP)
    before = lax.ppermute(high, "cuts", up)
    after = lax.ppermute(low, "cuts", [(j, i) for i, j in up])
    chip = (kept.astype(jnp.float32) + other.astype(jnp.float32)).astype(jnp.bfloat16)
    got = exchange(chip, GROUP_Y).reshape(NY, NZ * OWN, slabs, lanes)
    row = jnp.sum(got.astype(jnp.float32), axis=0).astype(jnp.bfloat16)
    row, before, after = lax.optimization_barrier((row, before, after))
    got = exchange(row, GROUP_Z).reshape(NZ, OWN, slabs, lanes)
    summed = jnp.sum(got.astype(jnp.float32), axis=0)
    residual = stat_weight * (measured - summed)
    resid_half = residual.astype(jnp.bfloat16)

    back = exchange(jnp.tile(resid_half, (NZ, 1, 1, 1)).reshape(NZ * OWN, slabs, lanes), GROUP_Z)
    back = lax.all_gather(back, "region", axis=0, tiled=True, axis_index_groups=GROUP_Y)
    theirs = lax.ppermute(back, "region", SWAP)

    padded = jnp.concatenate([before, image, after], axis=1)
    global_slice = lax.axis_index("cuts") * slabs + jnp.arange(slabs, dtype=jnp.int32)
    below = jnp.where((global_slice > 0)[None, :, None], image - padded[:, :-2, :], 0.0)
    above = jnp.where(
        (global_slice < slabs * cuts - 1)[None, :, None], image - padded[:, 2:, :], 0.0
    )
    start = image - smoothing_weight * (below + above) / precond
    updated = call(
        backward_kernel, "backproject", tables + (back, theirs, start, precond), [VM] * 4,
        jax.ShapeDtypeStruct(image.shape, jnp.float32),
        [
            pltpu.VMEM((rows, slabs, lanes), jnp.bfloat16),
            pltpu.VMEM((LOC, slabs, lanes), jnp.bfloat16),
        ],
        blocks, 2 * 2048 * slabs * lanes * lanes, 6 << 20,
    )
    return (updated, residual)


def solution(mesh):
    in_specs = (
        P("region", "cuts", None),
        P("region", "cuts", None),
        P(),
        P(),
        P("region", None),
        P("region", None),
        P("region", None),
        P(),
        P("region", "cuts", None),
        P("region", "cuts", None),
    )
    out_specs = (P("region", "cuts", None), P("region", "cuts", None))
    return jax.shard_map(
        per_device, mesh=mesh, in_specs=in_specs, out_specs=out_specs, check_vma=False
    )
```

time: 106 us -> 89 us (0.84)
  blocking collectives: 53 us -> 37.4 us
  local copies, waits for them, and re-layouts: 9.99 us -> 0.04 us
  waiting for transfers between devices: 5.25 us -> 12.1 us
  starting transfers between devices: 14.8 us -> 17.2 us
  other arithmetic: 1.33 us -> 3.39 us
  Pallas kernels: 19.7 us -> 17.8 us
    all_to_all x3 -> x2, blocking collectives: 41.9 us -> 26.5 us  [exchange(): lax.all_to_all(x, 'region', split_axis=0, concat_axis=0, tiled=True, axis...]
    unnamed x32 -> x8, local copies, waits for them, and re-layouts: 9.05 us -> 0.01 us
    all_to_all x0 -> x1, waiting for transfers between devices: none -> 8.6 us  [exchange(): lax.all_to_all(x, 'region', split_axis=0, concat_axis=0, tiled=True, axis...]
    all_to_all x0 -> x1, starting transfers between devices: none -> 3.62 us  [exchange(): lax.all_to_all(x, 'region', split_axis=0, concat_axis=0, tiled=True, axis...]
    ppermute x3, waiting for transfers between devices: 5.24 us -> 1.92 us  [the longest x1 1.91 us: per_device(): other = lax.ppermute(given, 'region', SWAP)]
    pallas_call x2, Pallas kernels: 19.7 us -> 17.8 us  [call(): pl.pallas_call(kernel, name=name, out_shape=out, in_specs=[ANYWHERE] * 6...]
    ppermute x1, waiting for transfers between devices: 0.01 us -> 1.59 us  [per_device(): theirs = lax.ppermute(back, 'region', SWAP)]
    reduce_sum x0 -> x1, other arithmetic: none -> 1.09 us  [per_device(): jnp.sum(jnp.where(mine[None, None, :], recv_map.transpose(2, 0, 1), 0), a...]
  transfers between devices with their start and end apart: 4 -> 5, of which waited for: 2 -> 3; matrix products, arithmetic and copies ran while one was open for 0% -> 1% of each run, Pallas kernels for 0% -> 0%
where the time goes in v2:
time: 89 us; the launch traced here: 88.6 us
  blocking collectives  37.4 us (42%)
  Pallas kernels  17.8 us (20%)
  starting transfers between devices  17.2 us (19%)
  waiting for transfers between devices  12.1 us (14%)
  other arithmetic  3.39 us (4%)
    all_to_all x2, blocking collectives, exchange(): lax.all_to_all(x, 'region', split_axis=0, concat_axis=0, tiled=True, axis...  26.5 us
    pallas_call x2, Pallas kernels, call(): pl.pallas_call(kernel, name=name, out_shape=out, in_specs=[ANYWHERE] * 6...  17.8 us
    all_gather x1, blocking collectives, per_device(): lax.all_gather(back, 'region', axis=0, tiled=True, axis_index_groups=GROU...  10.9 us
    all_to_all x1, waiting for transfers between devices, exchange(): lax.all_to_all(x, 'region', split_axis=0, concat_axis=0, tiled=True, axis...  8.6 us
    ppermute x1, starting transfers between devices, per_device(): theirs = lax.ppermute(back, 'region', SWAP)  6.93 us
    all_to_all x1, starting transfers between devices, exchange(): lax.all_to_all(x, 'region', split_axis=0, concat_axis=0, tiled=True, axis...  3.62 us
    ppermute x1, starting transfers between devices, per_device(): other = lax.ppermute(given, 'region', SWAP)  3.27 us
    ppermute x1, starting transfers between devices, per_device(): before = lax.ppermute(high, 'cuts', up)  2.07 us
  transfers between devices with their start and end apart: 5, of which 3 were waited for; matrix products, arithmetic and copies ran while one was open for 1% of the time, Pallas kernels for 0%

profile of v2, /device:TPU:1, one launch (start us, length us, event | category | flops | bytes accessed | tf_op | source)
XLA Modules:
  0.0 88.6 jit_solution(1872690531568882366)
XLA Ops:
  0.7 1.1 %select_reduce_fusion = s32[64,5]{0,1:T(8,128)S(1)} fusion(s32[64,64,5]{1,0,2:T(8,128)} %param.17, pred[64]{0:T(512)(128)(4,1)S(1)} %iota_compare_fusion), kind=kLoop, calls=%fused_computation.12 | loop fusion | flops 40640 | bytes 83264 | tf_op jit(solution)/shard_map/reduce_sum | solution.py:194
  1.8 8.7 %project.1 = (bf16[192,16,128]{2,1,0:T(8,128)(2,1)S(1)}, bf16[192,16,128]{2,1,0:T(8,128)(2,1)S(1)}, f32[64,1,128]{2,1,0:T(1,128)S(1)}, f32[64,1,128]{2,1,0:T(1,128)S(1)}) custom-call(s32[1,2048]{1,0:T(1,128)} %pixels.3, s32[1,2048]{1,0:T(1,128)} %slots.3, s32[1,64]{1,0:T(1,128)} %counts.3, s32[5,64]{1,0:T(8,128)S(1)} %add_bitcast_fusion.owner_rows, ...), custom_call_target="tpu_custom_call" | custom-call | flops 1073741824 | bytes 6291456 | tf_op jit(solution)/shard_map/project/pallas_call | solution.py:144
  10.5 3.3 %collective-permute-start = (bf16[192,16,128]{2,1,0:T(8,128)(2,1)S(1)}, bf16[192,16,128]{2,1,0:T(8,128)(2,1)S(1)}, u32[]{:S(2)}, u32[]{:S(2)}) collective-permute-start(bf16[192,16,128]{2,1,0:T(8,128)(2,1)S(1)} %get-tuple-element.10), channel_id=1, source_target_pairs={{0,1},{1,0},{2,3},{3,2},{4,5},{5,4},{6,7},{7,6},{8,9},{9,8},{10,11... | collective-permute-start | bytes 2359304 | tf_op jit(solution)/shard_map/ppermute | solution.py:215
  13.8 1.9 %collective-permute-done = bf16[192,16,128]{2,1,0:T(8,128)(2,1)S(1)} collective-permute-done((bf16[192,16,128]{2,1,0:T(8,128)(2,1)S(1)}, bf16[192,16,128]{2,1,0:T(8,128)(2,1)S(1)}, u32[]{:S(2)}, u32[]{:S(2)}) %collective-permute-start) | collective-permute-done | bytes 786464 | tf_op jit(solution)/shard_map/ppermute | solution.py:215
  15.7 1.1 %add_convert_fusion = bf16[192,16,128]{2,1,0:T(8,128)(2,1)} fusion(bf16[192,16,128]{2,1,0:T(8,128)(2,1)S(1)} %collective-permute-done, bf16[192,16,128]{2,1,0:T(8,128)(2,1)S(1)} %get-tuple-element.9), kind=kLoop, calls=%fused_computation | loop fusion | flops 1572864 | bytes 2359296 | tf_op jit(solution)/shard_map/convert_element_type | solution.py:218
  16.8 0.0 copy-start.2
  16.8 0.0 copy-start.3
  16.8 3.6 %all-to-all-start = ((bf16[192,16,128]{2,1,0:T(8,128)(2,1)}), bf16[192,16,128]{2,1,0:T(8,128)(2,1)S(1)}, u32[]{:S(2)}, u32[]{:S(2)}) async-start(bf16[192,16,128]{2,1,0:T(8,128)(2,1)} %add_convert_fusion), calls=%async_computation | async-start | bytes 1572864 | tf_op jit(solution)/shard_map/all_to_all | solution.py:179
  20.4 2.1 %collective-permute-start.1 = (f32[64,1,128]{2,1,0:T(1,128)S(1)}, f32[64,1,128]{2,1,0:T(1,128)S(1)}, u32[]{:S(2)}, u32[]{:S(2)}) collective-permute-start(f32[64,1,128]{2,1,0:T(1,128)S(1)} %get-tuple-element.11), channel_id=1, source_target_pairs={{0,64},{64,128},{128,192},{1,65},{65,129},{129,193},{2,66},{66,130... | collective-permute-start | bytes 98312 | tf_op jit(solution)/shard_map/ppermute | solution.py:216
  22.5 1.3 %collective-permute-start.2 = (f32[64,1,128]{2,1,0:T(1,128)S(1)}, f32[64,1,128]{2,1,0:T(1,128)S(1)}, u32[]{:S(2)}, u32[]{:S(2)}) collective-permute-start(f32[64,1,128]{2,1,0:T(1,128)S(1)} %get-tuple-element.12), channel_id=1, source_target_pairs={{64,0},{128,64},{192,128},{65,1},{129,65},{193,129},{66,2},{130,66... | collective-permute-start | bytes 98312 | tf_op jit(solution)/shard_map/ppermute | solution.py:217
  23.8 8.6 %all-to-all-done = bf16[192,16,128]{2,1,0:T(8,128)(2,1)S(1)} async-done(((bf16[192,16,128]{2,1,0:T(8,128)(2,1)}), bf16[192,16,128]{2,1,0:T(8,128)(2,1)S(1)}, u32[]{:S(2)}, u32[]{:S(2)}) %all-to-all-start) | async-done | bytes 786464 | tf_op jit(solution)/shard_map/all_to_all | solution.py:179
  32.4 0.0 copy-start
  32.4 0.0 copy-start.1
  32.4 0.2 reduce_sum.31
  32.6 0.0 collective-permute-done.1
  32.6 0.0 collective-permute-done.2
  32.6 15.5 %all_to_all.15 = bf16[48,16,128]{2,1,0:T(8,128)(2,1)S(1)} all-to-all(bf16[48,16,128]{2,1,0:T(8,128)(2,1)S(1)} %reduce_sum.31), channel_id=1, replica_groups={{0,8,16,24,32,40,48,56},{1,9,17,25,33,41,49,57},{2,10,18,26,34,42,50,58..., dimensions={0} | all-to-all | bytes 393216 | tf_op jit(solution)/shard_map/all_to_all | solution.py:179
  48.1 0.0 copy-done.2
  48.2 0.0 copy-done.3
  48.2 0.6 fusion.17
  48.8 11.0 %all_to_all.16 = bf16[48,16,128]{2,1,0:T(8,128)(2,1)S(1)} all-to-all(bf16[48,16,128]{2,1,0:T(8,128)(2,1)S(1)} %bitcast.7), channel_id=1, replica_groups={{0,8,16,24,32,40,48,56},{1,9,17,25,33,41,49,57},{2,10,18,26,34,42,50,58..., dimensions={0} | all-to-all | bytes 393216 | tf_op jit(solution)/shard_map/all_to_all | solution.py:179
  59.9 10.9 %all_gather.3.mine = bf16[192,16,128]{2,1,0:T(8,128)(2,1)S(1)} all-gather(bf16[48,16,128]{2,1,0:T(8,128)(2,1)S(1)} %all_to_all.16), channel_id=1, replica_groups={{0,2,4,6},{1,3,5,7},{8,10,12,14},{9,11,13,15},{16,18,20,22},{17,19,21,2..., dimensions={0}, use_global_device_ids=true | all-gather | bytes 983040 | tf_op jit(solution)/shard_map/all_gather | solution.py:228
  70.7 6.9 %collective-permute-start.3 = (bf16[192,16,128]{2,1,0:T(8,128)(2,1)S(1)}, bf16[192,16,128]{2,1,0:T(8,128)(2,1)S(1)}, u32[]{:S(2)}, u32[]{:S(2)}) collective-permute-start(bf16[192,16,128]{2,1,0:T(8,128)(2,1)S(1)} %all_gather.3.mine), channel_id=1, source_target_pairs={{0,1},{1,0},{2,3},{3,2},{4,5},{5,4},{6,7},{7,6},{8,9},{9,8},{10,11... | collective-permute-start | bytes 2359304 | tf_op jit(solution)/shard_map/ppermute | solution.py:229
  77.7 0.0 copy-done
  77.7 0.0 copy-done.1
  77.7 0.3 fusion.5.start
  78.0 1.6 %collective-permute-done.3.theirs = bf16[192,16,128]{2,1,0:T(8,128)(2,1)S(1)} collective-permute-done((bf16[192,16,128]{2,1,0:T(8,128)(2,1)S(1)}, bf16[192,16,128]{2,1,0:T(8,128)(2,1)S(1)}, u32[]{:S(2)}, u32[]{:S(2)}) %collective-permute-start.3) | collective-permute-done | bytes 786464 | tf_op jit(solution)/shard_map/ppermute | solution.py:229
  79.6 9.1 %backproject.1 = f32[64,16,128]{2,1,0:T(8,128)} custom-call(s32[1,2048]{1,0:T(1,128)} %pixels.3, s32[1,2048]{1,0:T(1,128)} %slots.3, s32[1,64]{1,0:T(1,128)} %counts.3, s32[5,64]{1,0:T(8,128)S(1)} %add_bitcast_fusion.owner_rows, s32[32]{0:T(128)} %subset.3, bf16[32,4,128,128]{3,2,1,0:T(8,128)(2,1)} %table.3, bf16[192,16,128]{2,1,0:T(8,128)(2,1)S(1)} %all_gather.3.mine, ...), custom_call_target="tpu_custom_call" | custom-call | flops 1073741824 | bytes 6291456 | tf_op jit(solution)/shard_map/backproject/pallas_call | solution.py:144
  (6 shorter events, 0.1 us)
Async XLA Ops:
  10.5 5.2 %collective-permute-start = (bf16[192,16,128]{2,1,0:T(8,128)(2,1)S(1)}, bf16[192,16,128]{2,1,0:T(8,128)(2,1)S(1)}, u32[]{:S(2)}, u32[]{:S(2)}) collective-permute-start(bf16[192,16,128]{2,1,0:T(8,128)(2,1)S(1)} %get-tuple-element.10), channel_id=1, source_target_pairs={{0,1},{1,0},{2,3},{3,2},{4,5},{5,4},{6,7},{7,6},{8,9},{9,8},{10,11... | collective-permute-start | bytes 2359304 | tf_op jit(solution)/shard_map/ppermute | solution.py:215
  16.8 31.3 %copy-start.2 = (f32[6,16,128]{2,1,0:T(8,128)S(1)}, f32[6,16,128]{2,1,0:T(8,128)}, u32[]{:S(2)}) copy-start(f32[6,16,128]{2,1,0:T(8,128)} %param.19) | copy-start | bytes 147460
  16.8 31.3 %copy-start.3 = (f32[6,16,128]{2,1,0:T(8,128)S(1)}, f32[6,16,128]{2,1,0:T(8,128)}, u32[]{:S(2)}) copy-start(f32[6,16,128]{2,1,0:T(8,128)} %param.18) | copy-start | bytes 147460
  16.8 15.6 %all-to-all-start = ((bf16[192,16,128]{2,1,0:T(8,128)(2,1)}), bf16[192,16,128]{2,1,0:T(8,128)(2,1)S(1)}, u32[]{:S(2)}, u32[]{:S(2)}) async-start(bf16[192,16,128]{2,1,0:T(8,128)(2,1)} %add_convert_fusion), calls=%async_computation | async-start | bytes 1572864 | tf_op jit(solution)/shard_map/all_to_all | solution.py:179
  20.4 12.1 %collective-permute-start.1 = (f32[64,1,128]{2,1,0:T(1,128)S(1)}, f32[64,1,128]{2,1,0:T(1,128)S(1)}, u32[]{:S(2)}, u32[]{:S(2)}) collective-permute-start(f32[64,1,128]{2,1,0:T(1,128)S(1)} %get-tuple-element.11), channel_id=1, source_target_pairs={{0,64},{64,128},{128,192},{1,65},{65,129},{129,193},{2,66},{66,130... | collective-permute-start | bytes 98312 | tf_op jit(solution)/shard_map/ppermute | solution.py:216
  22.5 10.1 %collective-permute-start.2 = (f32[64,1,128]{2,1,0:T(1,128)S(1)}, f32[64,1,128]{2,1,0:T(1,128)S(1)}, u32[]{:S(2)}, u32[]{:S(2)}) collective-permute-start(f32[64,1,128]{2,1,0:T(1,128)S(1)} %get-tuple-element.12), channel_id=1, source_target_pairs={{64,0},{128,64},{192,128},{65,1},{129,65},{193,129},{66,2},{130,66... | collective-permute-start | bytes 98312 | tf_op jit(solution)/shard_map/ppermute | solution.py:217
  32.4 45.2 %copy-start = (f32[64,16,128]{2,1,0:T(8,128)S(1)}, f32[64,16,128]{2,1,0:T(8,128)}, u32[]{:S(2)}) copy-start(f32[64,16,128]{2,1,0:T(8,128)} %precond.1) | copy-start | bytes 1572868
  32.4 45.2 %copy-start.1 = (f32[64,16,128]{2,1,0:T(8,128)S(1)}, f32[64,16,128]{2,1,0:T(8,128)}, u32[]{:S(2)}) copy-start(f32[64,16,128]{2,1,0:T(8,128)} %image.1) | copy-start | bytes 1572868
  70.7 8.8 %collective-permute-start.3 = (bf16[192,16,128]{2,1,0:T(8,128)(2,1)S(1)}, bf16[192,16,128]{2,1,0:T(8,128)(2,1)S(1)}, u32[]{:S(2)}, u32[]{:S(2)}) collective-permute-start(bf16[192,16,128]{2,1,0:T(8,128)(2,1)S(1)} %all_gather.3.mine), channel_id=1, source_target_pairs={{0,1},{1,0},{2,3},{3,2},{4,5},{5,4},{6,7},{7,6},{8,9},{9,8},{10,11... | collective-permute-start | bytes 2359304 | tf_op jit(solution)/shard_map/ppermute | solution.py:229

commit v3 on v2

--- a/solution.py
+++ b/solution.py
@@ -11,8 +11,9 @@
 CAP = 5
 NZ, NY, NC = 8, 4, 2
 smoothing_weight = 0.5
-NACC = 4
-WINDOWS = 4
+NACC = 6
+WINDOWS = 8
+TOGETHER = 4
 VMEM = 48 << 20
 LOC = 128
 SLABS = 16
@@ -31,13 +32,17 @@
 class Tables:
     def __init__(self, pixels, slots, counts, owner_rows, subset, table, scratch):
         (self.counts_s, self.owner_s, self.subset_s, self.rays, self.table_v,
-         self.sems, self.table_sems, self.window_sems) = scratch[:8]
-        self.windows = [scratch[8 + 2 * b : 10 + 2 * b] for b in range(WINDOWS)]
-        self.pixels, self.slots, self.table = pixels, slots, table
+         self.sems, self.table_sems, self.window_sems, pixels_v, slots_v) = scratch[:10]
+        self.staged = (pixels_v, slots_v)
+        self.windows = [scratch[10 + 2 * b : 12 + 2 * b] for b in range(WINDOWS)]
+        self.table = table
         self.small = [
             pltpu.make_async_copy(source, target, self.sems.at[i])
             for i, (source, target) in enumerate(
-                ((subset, self.subset_s), (counts, self.counts_s), (owner_rows, self.owner_s))
+                (
+                    (subset, self.subset_s), (pixels, pixels_v), (slots, slots_v),
+                    (counts, self.counts_s), (owner_rows, self.owner_s),
+                )
             )
         ]
 
@@ -45,7 +50,7 @@
         here = pl.ds(pl.multiple_of(a * LANES, LANES), LANES)
         return [
             pltpu.make_async_copy(source.at[:, here], target, self.window_sems.at[i, b])
-            for i, (source, target) in enumerate(zip((self.pixels, self.slots), self.windows[b]))
+            for i, (source, target) in enumerate(zip(self.staged, self.windows[b]))
         ]
 
     def footprints(self, row, a):
@@ -54,16 +59,22 @@
     def start(self, cleared):
         for copy in self.small:
             copy.start()
-        for b in range(WINDOWS):
-            for copy in self.window(b, b):
-                copy.start()
-        for ref in cleared:
+        half = len(cleared) // 2
+        for ref in cleared[:half]:
             ref[...] = jnp.zeros_like(ref)
         self.small[0].wait()
         for a in range(ANG):
             self.footprints(self.subset_s[a], a).start()
-        self.small[1].wait()
-        self.small[2].wait()
+        for copy, ref in zip(self.small[1:3], self.staged):
+            copy.wait()
+            ref[...] = ref[...] * SLABS
+        for ref in cleared[half:]:
+            ref[...] = jnp.zeros_like(ref)
+        for b in range(WINDOWS):
+            for copy in self.window(b, b):
+                copy.start()
+        self.small[3].wait()
+        self.small[4].wait()
         fill_rays(self.counts_s, self.owner_s, self.rays)
 
     def sweep(self, source, accs, take_slot, contract):
@@ -71,28 +82,33 @@
 
         @pl.loop(0, ANG // WINDOWS)
         def _(g):
-            for b in range(WINDOWS):
-                a = g * WINDOWS + b
-                for copy in self.window(a, b):
-                    copy.wait()
-                self.footprints(0, a).wait()
-                pixel, slot = self.windows[b]
-                take, put = (slot, pixel) if take_slot else (pixel, slot)
-                for shift in range(SHIFTS):
-                    base = shift * tiles
-                    x = jnp.concatenate([source[take[0, base + t]] for t in range(tiles)], axis=0)
-                    y = lax.dot_general(
-                        x, self.table_v[a, shift], (((1,), (contract,)), ((), ())),
-                        preferred_element_type=jnp.float32,
-                    )
-                    for t in range(tiles):
-                        acc = accs[t % NACC]
-                        acc[put[0, base + t]] += y[t * SLABS : (t + 1) * SLABS]
+            for first in range(0, WINDOWS, TOGETHER):
+                turn = range(first, first + TOGETHER)
+                for b in turn:
+                    for copy in self.window(g * WINDOWS + b, b):
+                        copy.wait()
+                    self.footprints(0, g * WINDOWS + b).wait()
+                for b in turn:
+                    pixel, slot = self.windows[b]
+                    take, put = (slot, pixel) if take_slot else (pixel, slot)
+                    for shift in range(SHIFTS):
+                        base = shift * tiles
+                        x = jnp.concatenate(
+                            [source[pl.ds(take[0, base + t], SLABS), :] for t in range(tiles)], axis=0
+                        ).astype(jnp.bfloat16)
+                        y = lax.dot_general(
+                            x, self.table_v[g * WINDOWS + b, shift],
+                            (((1,), (contract,)), ((), ())), preferred_element_type=jnp.float32,
+                        )
+                        for t in range(tiles):
+                            acc = accs[t % NACC]
+                            acc[pl.ds(put[0, base + t], SLABS), :] += y[t * SLABS : (t + 1) * SLABS]
 
                 @pl.when(g < ANG // WINDOWS - 1)
                 def _():
-                    for copy in self.window(a + WINDOWS, b):
-                        copy.start()
+                    for b in turn:
+                        for copy in self.window((g + 1) * WINDOWS + b, b):
+                            copy.start()
 
 
 def forward_kernel(pixels, slots, counts, owner_rows, subset, table, image, mine, theirs, low, high, *scratch):
@@ -103,14 +119,15 @@
     image_copy.start()
     tables.start((*accs, total))
     image_copy.wait()
-    xb[...] = image_v[...].astype(jnp.bfloat16)
+    xb[...] = image_v[...].astype(jnp.bfloat16).astype(jnp.float32).reshape(xb.shape)
     low[...] = image_v[:, :1, :]
     high[...] = image_v[:, SLABS - 1 :, :]
     tables.sweep(xb, accs, False, 1)
 
     @pl.loop(0, LOC, unroll=8)
     def _(j):
-        total[tables.rays[j]] += sum(acc[j] for acc in accs)
+        here = pl.ds(pl.multiple_of(j * SLABS, SLABS), SLABS)
+        total[tables.rays[j]] += sum(acc[here, :] for acc in accs)
 
     half = mine.shape[0]
     mine[...] = total[:half].astype(jnp.bfloat16)
@@ -128,10 +145,11 @@
 
     @pl.loop(0, LOC, unroll=8)
     def _(j):
-        slot_resid[j] = rb[tables.rays[j]]
+        here = pl.ds(pl.multiple_of(j * SLABS, SLABS), SLABS)
+        slot_resid[here, :] = rb[tables.rays[j]].astype(jnp.float32)
 
     tables.sweep(slot_resid, accs, True, 0)
-    out[...] = start[...] + sum(acc[...] for acc in accs) / precond[...]
+    out[...] = start[...] + sum(acc[...] for acc in accs).reshape(out.shape) / precond[...]
 
 
 VM = pl.BlockSpec(memory_space=pltpu.VMEM)
@@ -148,14 +166,16 @@
         in_specs=[ANYWHERE] * 6 + specs,
         out_specs=[VM] * len(out) if several else VM,
         scratch_shapes=dense
-        + [pltpu.VMEM((acc_rows, SLABS, LANES), jnp.float32)] * NACC
+        + [pltpu.VMEM((acc_rows * SLABS, LANES), jnp.float32)] * NACC
         + [pltpu.SMEM(operand.shape, jnp.int32) for operand in operands[2:5]]
         + [
             pltpu.SMEM((160,), jnp.int32),
             pltpu.VMEM((ANG,) + table.shape[1:], table.dtype),
-            pltpu.SemaphoreType.DMA((3,)),
+            pltpu.SemaphoreType.DMA((5,)),
             pltpu.SemaphoreType.DMA((ANG,)),
             pltpu.SemaphoreType.DMA((2, WINDOWS)),
+            pltpu.VMEM(operands[0].shape, jnp.int32),
+            pltpu.VMEM(operands[1].shape, jnp.int32),
         ]
         + [pltpu.SMEM((1, LANES), jnp.int32)] * (2 * WINDOWS),
         compiler_params=pltpu.CompilerParams(vmem_limit_bytes=VMEM),
@@ -204,7 +224,7 @@
         forward_kernel, "project", tables + (image,), [ANYWHERE], (local, local, edge, edge),
         [
             pltpu.VMEM((blocks, slabs, lanes), jnp.float32),
-            pltpu.VMEM((blocks, slabs, lanes), jnp.bfloat16),
+            pltpu.VMEM((blocks * slabs, lanes), jnp.float32),
             pltpu.VMEM((rows, slabs, lanes), jnp.float32),
             pltpu.SemaphoreType.DMA,
         ],
@@ -240,7 +260,7 @@
         jax.ShapeDtypeStruct(image.shape, jnp.float32),
         [
             pltpu.VMEM((rows, slabs, lanes), jnp.bfloat16),
-            pltpu.VMEM((LOC, slabs, lanes), jnp.bfloat16),
+            pltpu.VMEM((LOC * slabs, lanes), jnp.float32),
         ],
         blocks, 2 * 2048 * slabs * lanes * lanes, 6 << 20,
     )

time: 89 us -> 84.8 us (0.953)
  Pallas kernels: 17.8 us -> 13.6 us
    pallas_call x2, Pallas kernels: 17.8 us -> 13.6 us  [call(): pl.pallas_call(kernel, name=name, out_shape=out, in_specs=[ANYWHERE] * 6...]
where the time goes in v3:
time: 84.8 us; the launch traced here: 84.5 us
  blocking collectives  37.4 us (44%)
  starting transfers between devices  17.2 us (20%)
  Pallas kernels  13.6 us (16%)
  waiting for transfers between devices  12.1 us (14%)
  other arithmetic  3.39 us (4%)
    all_to_all x2, blocking collectives, exchange(): lax.all_to_all(x, 'region', split_axis=0, concat_axis=0, tiled=True, axis...  26.6 us
    pallas_call x2, Pallas kernels, call(): pl.pallas_call(kernel, name=name, out_shape=out, in_specs=[ANYWHERE] * 6...  13.6 us
    all_gather x1, blocking collectives, per_device(): lax.all_gather(back, 'region', axis=0, tiled=True, axis_index_groups=GROU...  10.9 us
    all_to_all x1, waiting for transfers between devices, exchange(): lax.all_to_all(x, 'region', split_axis=0, concat_axis=0, tiled=True, axis...  8.57 us
    ppermute x1, starting transfers between devices, per_device(): theirs = lax.ppermute(back, 'region', SWAP)  6.93 us
    all_to_all x1, starting transfers between devices, exchange(): lax.all_to_all(x, 'region', split_axis=0, concat_axis=0, tiled=True, axis...  3.62 us
    ppermute x1, starting transfers between devices, per_device(): other = lax.ppermute(given, 'region', SWAP)  3.28 us
    ppermute x1, starting transfers between devices, per_device(): before = lax.ppermute(high, 'cuts', up)  2.1 us
  transfers between devices with their start and end apart: 5, of which 3 were waited for; matrix products, arithmetic and copies ran while one was open for 1% of the time, Pallas kernels for 0%

profile of v3, /device:TPU:1, one launch (start us, length us, event | category | flops | bytes accessed | tf_op | source)
XLA Modules:
  0.0 84.5 jit_solution(11616417667892131907)
XLA Ops:
  0.7 1.1 %select_reduce_fusion = s32[64,5]{0,1:T(8,128)S(1)} fusion(s32[64,64,5]{1,0,2:T(8,128)} %param.17, pred[64]{0:T(512)(128)(4,1)S(1)} %iota_compare_fusion), kind=kLoop, calls=%fused_computation.12 | loop fusion | flops 40640 | bytes 83264 | tf_op jit(solution)/shard_map/reduce_sum | solution.py:214
  1.8 6.7 %project.1 = (bf16[192,16,128]{2,1,0:T(8,128)(2,1)S(1)}, bf16[192,16,128]{2,1,0:T(8,128)(2,1)S(1)}, f32[64,1,128]{2,1,0:T(1,128)S(1)}, f32[64,1,128]{2,1,0:T(1,128)S(1)}) custom-call(s32[1,2048]{1,0:T(1,128)} %pixels.3, s32[1,2048]{1,0:T(1,128)} %slots.3, s32[1,64]{1,0:T(1,128)} %counts.3, s32[5,64]{1,0:T(8,128)S(1)} %add_bitcast_fusion.owner_rows, ...), custom_call_target="tpu_custom_call" | custom-call | flops 1073741824 | bytes 6291456 | tf_op jit(solution)/shard_map/project/pallas_call | solution.py:162
  8.4 3.3 %collective-permute-start = (bf16[192,16,128]{2,1,0:T(8,128)(2,1)S(1)}, bf16[192,16,128]{2,1,0:T(8,128)(2,1)S(1)}, u32[]{:S(2)}, u32[]{:S(2)}) collective-permute-start(bf16[192,16,128]{2,1,0:T(8,128)(2,1)S(1)} %get-tuple-element.10), channel_id=1, source_target_pairs={{0,1},{1,0},{2,3},{3,2},{4,5},{5,4},{6,7},{7,6},{8,9},{9,8},{10,11... | collective-permute-start | bytes 2359304 | tf_op jit(solution)/shard_map/ppermute | solution.py:235
  11.7 1.9 %collective-permute-done = bf16[192,16,128]{2,1,0:T(8,128)(2,1)S(1)} collective-permute-done((bf16[192,16,128]{2,1,0:T(8,128)(2,1)S(1)}, bf16[192,16,128]{2,1,0:T(8,128)(2,1)S(1)}, u32[]{:S(2)}, u32[]{:S(2)}) %collective-permute-start) | collective-permute-done | bytes 786464 | tf_op jit(solution)/shard_map/ppermute | solution.py:235
  13.6 1.1 %add_convert_fusion = bf16[192,16,128]{2,1,0:T(8,128)(2,1)} fusion(bf16[192,16,128]{2,1,0:T(8,128)(2,1)S(1)} %collective-permute-done, bf16[192,16,128]{2,1,0:T(8,128)(2,1)S(1)} %get-tuple-element.9), kind=kLoop, calls=%fused_computation | loop fusion | flops 1572864 | bytes 2359296 | tf_op jit(solution)/shard_map/convert_element_type | solution.py:238
  14.8 0.0 copy-start.2
  14.8 0.0 copy-start.3
  14.8 3.6 %all-to-all-start = ((bf16[192,16,128]{2,1,0:T(8,128)(2,1)}), bf16[192,16,128]{2,1,0:T(8,128)(2,1)S(1)}, u32[]{:S(2)}, u32[]{:S(2)}) async-start(bf16[192,16,128]{2,1,0:T(8,128)(2,1)} %add_convert_fusion), calls=%async_computation | async-start | bytes 1572864 | tf_op jit(solution)/shard_map/all_to_all | solution.py:199
  18.4 2.1 %collective-permute-start.1 = (f32[64,1,128]{2,1,0:T(1,128)S(1)}, f32[64,1,128]{2,1,0:T(1,128)S(1)}, u32[]{:S(2)}, u32[]{:S(2)}) collective-permute-start(f32[64,1,128]{2,1,0:T(1,128)S(1)} %get-tuple-element.11), channel_id=1, source_target_pairs={{0,64},{64,128},{128,192},{1,65},{65,129},{129,193},{2,66},{66,130... | collective-permute-start | bytes 98312 | tf_op jit(solution)/shard_map/ppermute | solution.py:236
  20.5 1.3 %collective-permute-start.2 = (f32[64,1,128]{2,1,0:T(1,128)S(1)}, f32[64,1,128]{2,1,0:T(1,128)S(1)}, u32[]{:S(2)}, u32[]{:S(2)}) collective-permute-start(f32[64,1,128]{2,1,0:T(1,128)S(1)} %get-tuple-element.12), channel_id=1, source_target_pairs={{64,0},{128,64},{192,128},{65,1},{129,65},{193,129},{66,2},{130,66... | collective-permute-start | bytes 98312 | tf_op jit(solution)/shard_map/ppermute | solution.py:237
  21.8 8.6 %all-to-all-done = bf16[192,16,128]{2,1,0:T(8,128)(2,1)S(1)} async-done(((bf16[192,16,128]{2,1,0:T(8,128)(2,1)}), bf16[192,16,128]{2,1,0:T(8,128)(2,1)S(1)}, u32[]{:S(2)}, u32[]{:S(2)}) %all-to-all-start) | async-done | bytes 786464 | tf_op jit(solution)/shard_map/all_to_all | solution.py:199
  30.4 0.0 copy-start
  30.4 0.0 copy-start.1
  30.4 0.2 reduce_sum.31
  30.5 0.0 collective-permute-done.1
  30.6 0.0 collective-permute-done.2
  30.6 15.5 %all_to_all.15 = bf16[48,16,128]{2,1,0:T(8,128)(2,1)S(1)} all-to-all(bf16[48,16,128]{2,1,0:T(8,128)(2,1)S(1)} %reduce_sum.31), channel_id=1, replica_groups={{0,8,16,24,32,40,48,56},{1,9,17,25,33,41,49,57},{2,10,18,26,34,42,50,58..., dimensions={0} | all-to-all | bytes 393216 | tf_op jit(solution)/shard_map/all_to_all | solution.py:199
  46.1 0.0 copy-done.2
  46.1 0.0 copy-done.3
  46.2 0.6 fusion.17
  46.8 11.0 %all_to_all.16 = bf16[48,16,128]{2,1,0:T(8,128)(2,1)S(1)} all-to-all(bf16[48,16,128]{2,1,0:T(8,128)(2,1)S(1)} %bitcast.7), channel_id=1, replica_groups={{0,8,16,24,32,40,48,56},{1,9,17,25,33,41,49,57},{2,10,18,26,34,42,50,58..., dimensions={0} | all-to-all | bytes 393216 | tf_op jit(solution)/shard_map/all_to_all | solution.py:199
  57.9 10.9 %all_gather.3.mine = bf16[192,16,128]{2,1,0:T(8,128)(2,1)S(1)} all-gather(bf16[48,16,128]{2,1,0:T(8,128)(2,1)S(1)} %all_to_all.16), channel_id=1, replica_groups={{0,2,4,6},{1,3,5,7},{8,10,12,14},{9,11,13,15},{16,18,20,22},{17,19,21,2..., dimensions={0}, use_global_device_ids=true | all-gather | bytes 983040 | tf_op jit(solution)/shard_map/all_gather | solution.py:248
  68.7 6.9 %collective-permute-start.3 = (bf16[192,16,128]{2,1,0:T(8,128)(2,1)S(1)}, bf16[192,16,128]{2,1,0:T(8,128)(2,1)S(1)}, u32[]{:S(2)}, u32[]{:S(2)}) collective-permute-start(bf16[192,16,128]{2,1,0:T(8,128)(2,1)S(1)} %all_gather.3.mine), channel_id=1, source_target_pairs={{0,1},{1,0},{2,3},{3,2},{4,5},{5,4},{6,7},{7,6},{8,9},{9,8},{10,11... | collective-permute-start | bytes 2359304 | tf_op jit(solution)/shard_map/ppermute | solution.py:249
  75.6 0.0 copy-done
  75.7 0.0 copy-done.1
  75.7 0.3 fusion.5.start
  76.0 1.6 %collective-permute-done.3.theirs = bf16[192,16,128]{2,1,0:T(8,128)(2,1)S(1)} collective-permute-done((bf16[192,16,128]{2,1,0:T(8,128)(2,1)S(1)}, bf16[192,16,128]{2,1,0:T(8,128)(2,1)S(1)}, u32[]{:S(2)}, u32[]{:S(2)}) %collective-permute-start.3) | collective-permute-done | bytes 786464 | tf_op jit(solution)/shard_map/ppermute | solution.py:249
  77.6 6.9 %backproject.1 = f32[64,16,128]{2,1,0:T(8,128)} custom-call(s32[1,2048]{1,0:T(1,128)} %pixels.3, s32[1,2048]{1,0:T(1,128)} %slots.3, s32[1,64]{1,0:T(1,128)} %counts.3, s32[5,64]{1,0:T(8,128)S(1)} %add_bitcast_fusion.owner_rows, s32[32]{0:T(128)} %subset.3, bf16[32,4,128,128]{3,2,1,0:T(8,128)(2,1)} %table.3, bf16[192,16,128]{2,1,0:T(8,128)(2,1)S(1)} %all_gather.3.mine, ...), custom_call_target="tpu_custom_call" | custom-call | flops 1073741824 | bytes 6291456 | tf_op jit(solution)/shard_map/backproject/pallas_call | solution.py:162
  (6 shorter events, 0.1 us)
Async XLA Ops:
  8.4 5.2 %collective-permute-start = (bf16[192,16,128]{2,1,0:T(8,128)(2,1)S(1)}, bf16[192,16,128]{2,1,0:T(8,128)(2,1)S(1)}, u32[]{:S(2)}, u32[]{:S(2)}) collective-permute-start(bf16[192,16,128]{2,1,0:T(8,128)(2,1)S(1)} %get-tuple-element.10), channel_id=1, source_target_pairs={{0,1},{1,0},{2,3},{3,2},{4,5},{5,4},{6,7},{7,6},{8,9},{9,8},{10,11... | collective-permute-start | bytes 2359304 | tf_op jit(solution)/shard_map/ppermute | solution.py:235
  14.8 31.4 %copy-start.2 = (f32[6,16,128]{2,1,0:T(8,128)S(1)}, f32[6,16,128]{2,1,0:T(8,128)}, u32[]{:S(2)}) copy-start(f32[6,16,128]{2,1,0:T(8,128)} %param.19) | copy-start | bytes 147460
  14.8 31.4 %copy-start.3 = (f32[6,16,128]{2,1,0:T(8,128)S(1)}, f32[6,16,128]{2,1,0:T(8,128)}, u32[]{:S(2)}) copy-start(f32[6,16,128]{2,1,0:T(8,128)} %param.18) | copy-start | bytes 147460
  14.8 15.6 %all-to-all-start = ((bf16[192,16,128]{2,1,0:T(8,128)(2,1)}), bf16[192,16,128]{2,1,0:T(8,128)(2,1)S(1)}, u32[]{:S(2)}, u32[]{:S(2)}) async-start(bf16[192,16,128]{2,1,0:T(8,128)(2,1)} %add_convert_fusion), calls=%async_computation | async-start | bytes 1572864 | tf_op jit(solution)/shard_map/all_to_all | solution.py:199
  18.4 12.1 %collective-permute-start.1 = (f32[64,1,128]{2,1,0:T(1,128)S(1)}, f32[64,1,128]{2,1,0:T(1,128)S(1)}, u32[]{:S(2)}, u32[]{:S(2)}) collective-permute-start(f32[64,1,128]{2,1,0:T(1,128)S(1)} %get-tuple-element.11), channel_id=1, source_target_pairs={{0,64},{64,128},{128,192},{1,65},{65,129},{129,193},{2,66},{66,130... | collective-permute-start | bytes 98312 | tf_op jit(solution)/shard_map/ppermute | solution.py:236
  20.5 10.1 %collective-permute-start.2 = (f32[64,1,128]{2,1,0:T(1,128)S(1)}, f32[64,1,128]{2,1,0:T(1,128)S(1)}, u32[]{:S(2)}, u32[]{:S(2)}) collective-permute-start(f32[64,1,128]{2,1,0:T(1,128)S(1)} %get-tuple-element.12), channel_id=1, source_target_pairs={{64,0},{128,64},{192,128},{65,1},{129,65},{193,129},{66,2},{130,66... | collective-permute-start | bytes 98312 | tf_op jit(solution)/shard_map/ppermute | solution.py:237
  30.4 45.3 %copy-start = (f32[64,16,128]{2,1,0:T(8,128)S(1)}, f32[64,16,128]{2,1,0:T(8,128)}, u32[]{:S(2)}) copy-start(f32[64,16,128]{2,1,0:T(8,128)} %precond.1) | copy-start | bytes 1572868
  30.4 45.3 %copy-start.1 = (f32[64,16,128]{2,1,0:T(8,128)S(1)}, f32[64,16,128]{2,1,0:T(8,128)}, u32[]{:S(2)}) copy-start(f32[64,16,128]{2,1,0:T(8,128)} %image.1) | copy-start | bytes 1572868
  68.7 8.8 %collective-permute-start.3 = (bf16[192,16,128]{2,1,0:T(8,128)(2,1)S(1)}, bf16[192,16,128]{2,1,0:T(8,128)(2,1)S(1)}, u32[]{:S(2)}, u32[]{:S(2)}) collective-permute-start(bf16[192,16,128]{2,1,0:T(8,128)(2,1)S(1)} %all_gather.3.mine), channel_id=1, source_target_pairs={{0,1},{1,0},{2,3},{3,2},{4,5},{5,4},{6,7},{7,6},{8,9},{9,8},{10,11... | collective-permute-start | bytes 2359304 | tf_op jit(solution)/shard_map/ppermute | solution.py:249

commit v4 on v3

--- a/solution.py
+++ b/solution.py
@@ -190,8 +190,16 @@
     return (z * NY + y) * NC + c
 
 
-GROUP_Y = [[index_of(z, y, c) for y in range(NY)] for z in range(NZ) for c in range(NC)]
-GROUP_Z = [[index_of(z, y, c) for z in range(NZ)] for y in range(NY) for c in range(NC)]
+NL = 2
+NH = NZ // NL
+GROUP_Y = [
+    [index_of(h * NL + l, y, c) for y in range(NY) for l in range(NL)]
+    for h in range(NH) for c in range(NC)
+]
+GROUP_Z = [
+    [index_of(h * NL + l, y, c) for h in range(NH)]
+    for l in range(NL) for y in range(NY) for c in range(NC)
+]
 SWAP = [(i, i ^ 1) for i in range(NZ * NY * NC)]
 
 
@@ -209,7 +217,7 @@
     core = me % NC
     owners = jnp.arange(NZ * NY * NC, dtype=jnp.int32)
     oz, oy, oc = owners // (NY * NC), owners // NC % NY, owners % NC
-    place = (((oc ^ core) * NY + oy) * NZ + oz) * OWN
+    place = ((((oc ^ core) * NY + oy) * NL + oz % NL) * NH + oz // NL) * OWN
     mine = jnp.arange(NZ * NY * NC, dtype=jnp.int32) == me
     owner_rows = place[None, :] + jnp.sum(
         jnp.where(mine[None, None, :], recv_map.transpose(2, 0, 1), 0), axis=2
@@ -236,16 +244,16 @@
     before = lax.ppermute(high, "cuts", up)
     after = lax.ppermute(low, "cuts", [(j, i) for i, j in up])
     chip = (kept.astype(jnp.float32) + other.astype(jnp.float32)).astype(jnp.bfloat16)
-    got = exchange(chip, GROUP_Y).reshape(NY, NZ * OWN, slabs, lanes)
+    got = exchange(chip, GROUP_Y).reshape(NY * NL, NH * OWN, slabs, lanes)
     row = jnp.sum(got.astype(jnp.float32), axis=0).astype(jnp.bfloat16)
     row, before, after = lax.optimization_barrier((row, before, after))
-    got = exchange(row, GROUP_Z).reshape(NZ, OWN, slabs, lanes)
+    got = exchange(row, GROUP_Z).reshape(NH, OWN, slabs, lanes)
     summed = jnp.sum(got.astype(jnp.float32), axis=0)
     residual = stat_weight * (measured - summed)
     resid_half = residual.astype(jnp.bfloat16)
 
-    back = exchange(jnp.tile(resid_half, (NZ, 1, 1, 1)).reshape(NZ * OWN, slabs, lanes), GROUP_Z)
-    back = lax.all_gather(back, "region", axis=0, tiled=True, axis_index_groups=GROUP_Y)
+    back = exchange(jnp.tile(resid_half, (NH, 1, 1)), GROUP_Z)
+    back = exchange(jnp.tile(back, (NY * NL, 1, 1)), GROUP_Y)
     theirs = lax.ppermute(back, "region", SWAP)
 
     padded = jnp.concatenate([before, image, after], axis=1)

time: 84.8 us -> 82.4 us (0.972)
  blocking collectives: 37.4 us -> 36.2 us
  waiting for transfers between devices: 12.1 us -> 11.1 us
    all_gather x1 -> x0, blocking collectives: 10.9 us -> none  [per_device(): lax.all_gather(back, 'region', axis=0, tiled=True, axis_index_groups=GROU...]
    all_to_all x2 -> x3, blocking collectives: 26.6 us -> 36.2 us  [exchange(): lax.all_to_all(x, 'region', split_axis=0, concat_axis=0, tiled=True, axis...]
    ppermute x1, starting transfers between devices: 6.93 us -> 5.23 us  [per_device(): theirs = lax.ppermute(back, 'region', SWAP)]
    ppermute x1, starting transfers between devices: 2.1 us -> 3.12 us  [per_device(): before = lax.ppermute(high, 'cuts', up)]
    all_to_all x1, waiting for transfers between devices: 8.57 us -> 7.61 us  [exchange(): lax.all_to_all(x, 'region', split_axis=0, concat_axis=0, tiled=True, axis...]
where the time goes in v4:
time: 82.4 us; the launch traced here: 82 us
  blocking collectives  36.2 us (44%)
  starting transfers between devices  16.9 us (21%)
  Pallas kernels  13.6 us (17%)
  waiting for transfers between devices  11.1 us (13%)
  other arithmetic  3.32 us (4%)
    all_to_all x3, blocking collectives, exchange(): lax.all_to_all(x, 'region', split_axis=0, concat_axis=0, tiled=True, axis...  36.2 us
    pallas_call x2, Pallas kernels, call(): pl.pallas_call(kernel, name=name, out_shape=out, in_specs=[ANYWHERE] * 6...  13.6 us
    all_to_all x1, waiting for transfers between devices, exchange(): lax.all_to_all(x, 'region', split_axis=0, concat_axis=0, tiled=True, axis...  7.61 us
    ppermute x1, starting transfers between devices, per_device(): theirs = lax.ppermute(back, 'region', SWAP)  5.23 us
    all_to_all x1, starting transfers between devices, exchange(): lax.all_to_all(x, 'region', split_axis=0, concat_axis=0, tiled=True, axis...  3.97 us
    ppermute x1, starting transfers between devices, per_device(): other = lax.ppermute(given, 'region', SWAP)  3.28 us
    ppermute x1, starting transfers between devices, per_device(): before = lax.ppermute(high, 'cuts', up)  3.12 us
    ppermute x1, waiting for transfers between devices, per_device(): other = lax.ppermute(given, 'region', SWAP)  1.91 us
  transfers between devices with their start and end apart: 5, of which 3 were waited for; matrix products, arithmetic and copies ran while one was open for 1% of the time, Pallas kernels for 0%

profile of v4, /device:TPU:1, one launch (start us, length us, event | category | flops | bytes accessed | tf_op | source)
XLA Modules:
  0.0 82.0 jit_solution(17932862239972933301)
XLA Ops:
  0.7 1.1 %select_reduce_fusion = s32[64,5]{0,1:T(8,128)S(1)} fusion(s32[64,64,5]{1,0,2:T(8,128)} %param.17, pred[64]{0:T(512)(128)(4,1)S(1)} %iota_compare_fusion), kind=kLoop, calls=%fused_computation.12 | loop fusion | flops 40640 | bytes 83264 | tf_op jit(solution)/shard_map/reduce_sum | solution.py:222
  1.8 6.7 %project.1 = (bf16[192,16,128]{2,1,0:T(8,128)(2,1)S(1)}, bf16[192,16,128]{2,1,0:T(8,128)(2,1)S(1)}, f32[64,1,128]{2,1,0:T(1,128)S(1)}, f32[64,1,128]{2,1,0:T(1,128)S(1)}) custom-call(s32[1,2048]{1,0:T(1,128)} %pixels.3, s32[1,2048]{1,0:T(1,128)} %slots.3, s32[1,64]{1,0:T(1,128)} %counts.3, s32[5,64]{1,0:T(8,128)S(1)} %add_bitcast_fusion.owner_rows, ...), custom_call_target="tpu_custom_call" | custom-call | flops 1073741824 | bytes 6291456 | tf_op jit(solution)/shard_map/project/pallas_call | solution.py:162
  8.5 3.3 %collective-permute-start = (bf16[192,16,128]{2,1,0:T(8,128)(2,1)S(1)}, bf16[192,16,128]{2,1,0:T(8,128)(2,1)S(1)}, u32[]{:S(2)}, u32[]{:S(2)}) collective-permute-start(bf16[192,16,128]{2,1,0:T(8,128)(2,1)S(1)} %get-tuple-element.10), channel_id=1, source_target_pairs={{0,1},{1,0},{2,3},{3,2},{4,5},{5,4},{6,7},{7,6},{8,9},{9,8},{10,11... | collective-permute-start | bytes 2359304 | tf_op jit(solution)/shard_map/ppermute | solution.py:243
  11.7 1.9 %collective-permute-done = bf16[192,16,128]{2,1,0:T(8,128)(2,1)S(1)} collective-permute-done((bf16[192,16,128]{2,1,0:T(8,128)(2,1)S(1)}, bf16[192,16,128]{2,1,0:T(8,128)(2,1)S(1)}, u32[]{:S(2)}, u32[]{:S(2)}) %collective-permute-start) | collective-permute-done | bytes 786464 | tf_op jit(solution)/shard_map/ppermute | solution.py:243
  13.6 1.1 %add_convert_fusion = bf16[192,16,128]{2,1,0:T(8,128)(2,1)} fusion(bf16[192,16,128]{2,1,0:T(8,128)(2,1)S(1)} %collective-permute-done, bf16[192,16,128]{2,1,0:T(8,128)(2,1)S(1)} %get-tuple-element.9), kind=kLoop, calls=%fused_computation | loop fusion | flops 1572864 | bytes 2359296 | tf_op jit(solution)/shard_map/convert_element_type | solution.py:246
  14.8 0.0 copy-start.2
  14.8 0.0 copy-start.3
  14.8 4.0 %all-to-all-start = ((bf16[192,16,128]{2,1,0:T(8,128)(2,1)}), bf16[192,16,128]{2,1,0:T(8,128)(2,1)S(1)}, u32[]{:S(2)}, u32[]{:S(2)}) async-start(bf16[192,16,128]{2,1,0:T(8,128)(2,1)} %add_convert_fusion), calls=%async_computation | async-start | bytes 1572864 | tf_op jit(solution)/shard_map/all_to_all | solution.py:207
  18.7 3.1 %collective-permute-start.1 = (f32[64,1,128]{2,1,0:T(1,128)S(1)}, f32[64,1,128]{2,1,0:T(1,128)S(1)}, u32[]{:S(2)}, u32[]{:S(2)}) collective-permute-start(f32[64,1,128]{2,1,0:T(1,128)S(1)} %get-tuple-element.11), channel_id=1, source_target_pairs={{0,64},{64,128},{128,192},{1,65},{65,129},{129,193},{2,66},{66,130... | collective-permute-start | bytes 98312 | tf_op jit(solution)/shard_map/ppermute | solution.py:244
  21.9 1.3 %collective-permute-start.2 = (f32[64,1,128]{2,1,0:T(1,128)S(1)}, f32[64,1,128]{2,1,0:T(1,128)S(1)}, u32[]{:S(2)}, u32[]{:S(2)}) collective-permute-start(f32[64,1,128]{2,1,0:T(1,128)S(1)} %get-tuple-element.12), channel_id=1, source_target_pairs={{64,0},{128,64},{192,128},{65,1},{129,65},{193,129},{66,2},{130,66... | collective-permute-start | bytes 98312 | tf_op jit(solution)/shard_map/ppermute | solution.py:245
  23.2 7.6 %all-to-all-done = bf16[192,16,128]{2,1,0:T(8,128)(2,1)S(1)} async-done(((bf16[192,16,128]{2,1,0:T(8,128)(2,1)}), bf16[192,16,128]{2,1,0:T(8,128)(2,1)S(1)}, u32[]{:S(2)}, u32[]{:S(2)}) %all-to-all-start) | async-done | bytes 786464 | tf_op jit(solution)/shard_map/all_to_all | solution.py:207
  30.8 0.1 reduce_sum.31
  30.9 0.0 collective-permute-done.1
  30.9 0.0 collective-permute-done.2
  30.9 14.2 %all_to_all.20 = bf16[24,16,128]{2,1,0:T(8,128)(2,1)S(1)} all-to-all(bf16[24,16,128]{2,1,0:T(8,128)(2,1)S(1)} %reduce_sum.31), channel_id=1, replica_groups={{0,16,32,48},{1,17,33,49},{2,18,34,50},{3,19,35,51},{4,20,36,52},{5,21,..., dimensions={0} | all-to-all | bytes 196608 | tf_op jit(solution)/shard_map/all_to_all | solution.py:207
  45.2 0.0 copy-start
  45.2 0.0 copy-start.1
  45.2 0.0 copy-done.2
  45.2 0.0 copy-done.3
  45.2 0.6 fusion.16
  45.9 9.4 %all_to_all.21 = bf16[24,16,128]{2,1,0:T(8,128)(2,1)S(1)} all-to-all(bf16[24,16,128]{2,1,0:T(8,128)(2,1)S(1)} %bitcast.10), channel_id=1, replica_groups={{0,16,32,48},{1,17,33,49},{2,18,34,50},{3,19,35,51},{4,20,36,52},{5,21,..., dimensions={0} | all-to-all | bytes 196608 | tf_op jit(solution)/shard_map/all_to_all | solution.py:207
  55.3 0.1 tile.20
  55.4 12.5 %all_to_all.22.mine = bf16[192,16,128]{2,1,0:T(8,128)(2,1)S(1)} all-to-all(bf16[192,16,128]{2,1,0:T(8,128)(2,1)S(1)} %bitcast.8), channel_id=1, replica_groups={{0,8,2,10,4,12,6,14},{1,9,3,11,5,13,7,15},{16,24,18,26,20,28,22,30},{17..., dimensions={0} | all-to-all | bytes 1572864 | tf_op jit(solution)/shard_map/all_to_all | solution.py:207
  67.9 5.2 %collective-permute-start.3 = (bf16[192,16,128]{2,1,0:T(8,128)(2,1)S(1)}, bf16[192,16,128]{2,1,0:T(8,128)(2,1)S(1)}, u32[]{:S(2)}, u32[]{:S(2)}) collective-permute-start(bf16[192,16,128]{2,1,0:T(8,128)(2,1)S(1)} %all_to_all.22.mine), channel_id=1, source_target_pairs={{0,1},{1,0},{2,3},{3,2},{4,5},{5,4},{6,7},{7,6},{8,9},{9,8},{10,11... | collective-permute-start | bytes 2359304 | tf_op jit(solution)/shard_map/ppermute | solution.py:257
  73.1 0.0 copy-done
  73.1 0.0 copy-done.1
  73.1 0.3 fusion.5.start
  73.5 1.6 %collective-permute-done.3.theirs = bf16[192,16,128]{2,1,0:T(8,128)(2,1)S(1)} collective-permute-done((bf16[192,16,128]{2,1,0:T(8,128)(2,1)S(1)}, bf16[192,16,128]{2,1,0:T(8,128)(2,1)S(1)}, u32[]{:S(2)}, u32[]{:S(2)}) %collective-permute-start.3) | collective-permute-done | bytes 786464 | tf_op jit(solution)/shard_map/ppermute | solution.py:257
  75.0 6.9 %backproject.1 = f32[64,16,128]{2,1,0:T(8,128)} custom-call(s32[1,2048]{1,0:T(1,128)} %pixels.3, s32[1,2048]{1,0:T(1,128)} %slots.3, s32[1,64]{1,0:T(1,128)} %counts.3, s32[5,64]{1,0:T(8,128)S(1)} %add_bitcast_fusion.owner_rows, s32[32]{0:T(128)} %subset.3, bf16[32,4,128,128]{3,2,1,0:T(8,128)(2,1)} %table.3, bf16[192,16,128]{2,1,0:T(8,128)(2,1)S(1)} %all_to_all.22.mine, ...), custom_call_target="tpu_custom_call" | custom-call | flops 1073741824 | bytes 6291456 | tf_op jit(solution)/shard_map/backproject/pallas_call | solution.py:162
  (6 shorter events, 0.1 us)
Async XLA Ops:
  8.5 5.2 %collective-permute-start = (bf16[192,16,128]{2,1,0:T(8,128)(2,1)S(1)}, bf16[192,16,128]{2,1,0:T(8,128)(2,1)S(1)}, u32[]{:S(2)}, u32[]{:S(2)}) collective-permute-start(bf16[192,16,128]{2,1,0:T(8,128)(2,1)S(1)} %get-tuple-element.10), channel_id=1, source_target_pairs={{0,1},{1,0},{2,3},{3,2},{4,5},{5,4},{6,7},{7,6},{8,9},{9,8},{10,11... | collective-permute-start | bytes 2359304 | tf_op jit(solution)/shard_map/ppermute | solution.py:243
  14.8 30.4 %copy-start.2 = (f32[6,16,128]{2,1,0:T(8,128)S(1)}, f32[6,16,128]{2,1,0:T(8,128)}, u32[]{:S(2)}) copy-start(f32[6,16,128]{2,1,0:T(8,128)} %param.19) | copy-start | bytes 147460
  14.8 30.4 %copy-start.3 = (f32[6,16,128]{2,1,0:T(8,128)S(1)}, f32[6,16,128]{2,1,0:T(8,128)}, u32[]{:S(2)}) copy-start(f32[6,16,128]{2,1,0:T(8,128)} %param.18) | copy-start | bytes 147460
  14.8 16.0 %all-to-all-start = ((bf16[192,16,128]{2,1,0:T(8,128)(2,1)}), bf16[192,16,128]{2,1,0:T(8,128)(2,1)S(1)}, u32[]{:S(2)}, u32[]{:S(2)}) async-start(bf16[192,16,128]{2,1,0:T(8,128)(2,1)} %add_convert_fusion), calls=%async_computation | async-start | bytes 1572864 | tf_op jit(solution)/shard_map/all_to_all | solution.py:207
  18.7 12.2 %collective-permute-start.1 = (f32[64,1,128]{2,1,0:T(1,128)S(1)}, f32[64,1,128]{2,1,0:T(1,128)S(1)}, u32[]{:S(2)}, u32[]{:S(2)}) collective-permute-start(f32[64,1,128]{2,1,0:T(1,128)S(1)} %get-tuple-element.11), channel_id=1, source_target_pairs={{0,64},{64,128},{128,192},{1,65},{65,129},{129,193},{2,66},{66,130... | collective-permute-start | bytes 98312 | tf_op jit(solution)/shard_map/ppermute | solution.py:244
  21.9 9.0 %collective-permute-start.2 = (f32[64,1,128]{2,1,0:T(1,128)S(1)}, f32[64,1,128]{2,1,0:T(1,128)S(1)}, u32[]{:S(2)}, u32[]{:S(2)}) collective-permute-start(f32[64,1,128]{2,1,0:T(1,128)S(1)} %get-tuple-element.12), channel_id=1, source_target_pairs={{64,0},{128,64},{192,128},{65,1},{129,65},{193,129},{66,2},{130,66... | collective-permute-start | bytes 98312 | tf_op jit(solution)/shard_map/ppermute | solution.py:245
  45.2 28.0 %copy-start = (f32[64,16,128]{2,1,0:T(8,128)S(1)}, f32[64,16,128]{2,1,0:T(8,128)}, u32[]{:S(2)}) copy-start(f32[64,16,128]{2,1,0:T(8,128)} %precond.1) | copy-start | bytes 1572868
  45.2 28.0 %copy-start.1 = (f32[64,16,128]{2,1,0:T(8,128)S(1)}, f32[64,16,128]{2,1,0:T(8,128)}, u32[]{:S(2)}) copy-start(f32[64,16,128]{2,1,0:T(8,128)} %image.1) | copy-start | bytes 1572868
  67.9 7.1 %collective-permute-start.3 = (bf16[192,16,128]{2,1,0:T(8,128)(2,1)S(1)}, bf16[192,16,128]{2,1,0:T(8,128)(2,1)S(1)}, u32[]{:S(2)}, u32[]{:S(2)}) collective-permute-start(bf16[192,16,128]{2,1,0:T(8,128)(2,1)S(1)} %all_to_all.22.mine), channel_id=1, source_target_pairs={{0,1},{1,0},{2,3},{3,2},{4,5},{5,4},{6,7},{7,6},{8,9},{9,8},{10,11... | collective-permute-start | bytes 2359304 | tf_op jit(solution)/shard_map/ppermute | solution.py:257

commit v5 on v4

--- a/solution.py
+++ b/solution.py
@@ -12,8 +12,8 @@
 NZ, NY, NC = 8, 4, 2
 smoothing_weight = 0.5
 NACC = 6
-WINDOWS = 8
-TOGETHER = 4
+WINDOWS = 16
+TOGETHER = 8
 VMEM = 48 << 20
 LOC = 128
 SLABS = 16

time: 82.4 us -> 82.4 us (level)
  no operation moved by 1% of the time
where the time goes in v5:
time: 82.4 us; the launch traced here: 82 us
  blocking collectives  36.2 us (44%)
  starting transfers between devices  16.9 us (21%)
  Pallas kernels  13.6 us (17%)
  waiting for transfers between devices  11.1 us (13%)
  other arithmetic  3.32 us (4%)
    all_to_all x3, blocking collectives, exchange(): lax.all_to_all(x, 'region', split_axis=0, concat_axis=0, tiled=True, axis...  36.2 us
    pallas_call x2, Pallas kernels, call(): pl.pallas_call(kernel, name=name, out_shape=out, in_specs=[ANYWHERE] * 6...  13.6 us
    all_to_all x1, waiting for transfers between devices, exchange(): lax.all_to_all(x, 'region', split_axis=0, concat_axis=0, tiled=True, axis...  7.62 us
    ppermute x1, starting transfers between devices, per_device(): theirs = lax.ppermute(back, 'region', SWAP)  5.23 us
    all_to_all x1, starting transfers between devices, exchange(): lax.all_to_all(x, 'region', split_axis=0, concat_axis=0, tiled=True, axis...  3.96 us
    ppermute x1, starting transfers between devices, per_device(): other = lax.ppermute(given, 'region', SWAP)  3.32 us
    ppermute x1, starting transfers between devices, per_device(): before = lax.ppermute(high, 'cuts', up)  3.11 us
    ppermute x1, waiting for transfers between devices, per_device(): other = lax.ppermute(given, 'region', SWAP)  1.91 us
  transfers between devices with their start and end apart: 5, of which 3 were waited for; matrix products, arithmetic and copies ran while one was open for 1% of the time, Pallas kernels for 0%

profile of v5, /device:TPU:1, one launch (start us, length us, event | category | flops | bytes accessed | tf_op | source)
XLA Modules:
  0.0 82.0 jit_solution(651072595780433306)
XLA Ops:
  0.7 1.1 %select_reduce_fusion = s32[64,5]{0,1:T(8,128)S(1)} fusion(s32[64,64,5]{1,0,2:T(8,128)} %param.17, pred[64]{0:T(512)(128)(4,1)S(1)} %iota_compare_fusion), kind=kLoop, calls=%fused_computation.12 | loop fusion | flops 40640 | bytes 83264 | tf_op jit(solution)/shard_map/reduce_sum | solution.py:222
  1.8 6.7 %project.1 = (bf16[192,16,128]{2,1,0:T(8,128)(2,1)S(1)}, bf16[192,16,128]{2,1,0:T(8,128)(2,1)S(1)}, f32[64,1,128]{2,1,0:T(1,128)S(1)}, f32[64,1,128]{2,1,0:T(1,128)S(1)}) custom-call(s32[1,2048]{1,0:T(1,128)} %pixels.3, s32[1,2048]{1,0:T(1,128)} %slots.3, s32[1,64]{1,0:T(1,128)} %counts.3, s32[5,64]{1,0:T(8,128)S(1)} %add_bitcast_fusion.owner_rows, ...), custom_call_target="tpu_custom_call" | custom-call | flops 1073741824 | bytes 6291456 | tf_op jit(solution)/shard_map/project/pallas_call | solution.py:162
  8.5 3.3 %collective-permute-start = (bf16[192,16,128]{2,1,0:T(8,128)(2,1)S(1)}, bf16[192,16,128]{2,1,0:T(8,128)(2,1)S(1)}, u32[]{:S(2)}, u32[]{:S(2)}) collective-permute-start(bf16[192,16,128]{2,1,0:T(8,128)(2,1)S(1)} %get-tuple-element.10), channel_id=1, source_target_pairs={{0,1},{1,0},{2,3},{3,2},{4,5},{5,4},{6,7},{7,6},{8,9},{9,8},{10,11... | collective-permute-start | bytes 2359304 | tf_op jit(solution)/shard_map/ppermute | solution.py:243
  11.8 1.9 %collective-permute-done = bf16[192,16,128]{2,1,0:T(8,128)(2,1)S(1)} collective-permute-done((bf16[192,16,128]{2,1,0:T(8,128)(2,1)S(1)}, bf16[192,16,128]{2,1,0:T(8,128)(2,1)S(1)}, u32[]{:S(2)}, u32[]{:S(2)}) %collective-permute-start) | collective-permute-done | bytes 786464 | tf_op jit(solution)/shard_map/ppermute | solution.py:243
  13.8 1.1 %add_convert_fusion = bf16[192,16,128]{2,1,0:T(8,128)(2,1)} fusion(bf16[192,16,128]{2,1,0:T(8,128)(2,1)S(1)} %collective-permute-done, bf16[192,16,128]{2,1,0:T(8,128)(2,1)S(1)} %get-tuple-element.9), kind=kLoop, calls=%fused_computation | loop fusion | flops 1572864 | bytes 2359296 | tf_op jit(solution)/shard_map/convert_element_type | solution.py:246
  14.9 0.0 copy-start.2
  14.9 0.0 copy-start.3
  14.9 4.0 %all-to-all-start = ((bf16[192,16,128]{2,1,0:T(8,128)(2,1)}), bf16[192,16,128]{2,1,0:T(8,128)(2,1)S(1)}, u32[]{:S(2)}, u32[]{:S(2)}) async-start(bf16[192,16,128]{2,1,0:T(8,128)(2,1)} %add_convert_fusion), calls=%async_computation | async-start | bytes 1572864 | tf_op jit(solution)/shard_map/all_to_all | solution.py:207
  18.8 3.1 %collective-permute-start.1 = (f32[64,1,128]{2,1,0:T(1,128)S(1)}, f32[64,1,128]{2,1,0:T(1,128)S(1)}, u32[]{:S(2)}, u32[]{:S(2)}) collective-permute-start(f32[64,1,128]{2,1,0:T(1,128)S(1)} %get-tuple-element.11), channel_id=1, source_target_pairs={{0,64},{64,128},{128,192},{1,65},{65,129},{129,193},{2,66},{66,130... | collective-permute-start | bytes 98312 | tf_op jit(solution)/shard_map/ppermute | solution.py:244
  22.0 1.3 %collective-permute-start.2 = (f32[64,1,128]{2,1,0:T(1,128)S(1)}, f32[64,1,128]{2,1,0:T(1,128)S(1)}, u32[]{:S(2)}, u32[]{:S(2)}) collective-permute-start(f32[64,1,128]{2,1,0:T(1,128)S(1)} %get-tuple-element.12), channel_id=1, source_target_pairs={{64,0},{128,64},{192,128},{65,1},{129,65},{193,129},{66,2},{130,66... | collective-permute-start | bytes 98312 | tf_op jit(solution)/shard_map/ppermute | solution.py:245
  23.3 7.6 %all-to-all-done = bf16[192,16,128]{2,1,0:T(8,128)(2,1)S(1)} async-done(((bf16[192,16,128]{2,1,0:T(8,128)(2,1)}), bf16[192,16,128]{2,1,0:T(8,128)(2,1)S(1)}, u32[]{:S(2)}, u32[]{:S(2)}) %all-to-all-start) | async-done | bytes 786464 | tf_op jit(solution)/shard_map/all_to_all | solution.py:207
  30.9 0.1 reduce_sum.31
  31.0 0.0 collective-permute-done.1
  31.0 0.0 collective-permute-done.2
  31.0 14.2 %all_to_all.20 = bf16[24,16,128]{2,1,0:T(8,128)(2,1)S(1)} all-to-all(bf16[24,16,128]{2,1,0:T(8,128)(2,1)S(1)} %reduce_sum.31), channel_id=1, replica_groups={{0,16,32,48},{1,17,33,49},{2,18,34,50},{3,19,35,51},{4,20,36,52},{5,21,..., dimensions={0} | all-to-all | bytes 196608 | tf_op jit(solution)/shard_map/all_to_all | solution.py:207
  45.2 0.0 copy-start
  45.2 0.0 copy-start.1
  45.3 0.0 copy-done.2
  45.3 0.0 copy-done.3
  45.3 0.6 fusion.16
  45.9 9.4 %all_to_all.21 = bf16[24,16,128]{2,1,0:T(8,128)(2,1)S(1)} all-to-all(bf16[24,16,128]{2,1,0:T(8,128)(2,1)S(1)} %bitcast.10), channel_id=1, replica_groups={{0,16,32,48},{1,17,33,49},{2,18,34,50},{3,19,35,51},{4,20,36,52},{5,21,..., dimensions={0} | all-to-all | bytes 196608 | tf_op jit(solution)/shard_map/all_to_all | solution.py:207
  55.4 0.1 tile.20
  55.5 12.5 %all_to_all.22.mine = bf16[192,16,128]{2,1,0:T(8,128)(2,1)S(1)} all-to-all(bf16[192,16,128]{2,1,0:T(8,128)(2,1)S(1)} %bitcast.8), channel_id=1, replica_groups={{0,8,2,10,4,12,6,14},{1,9,3,11,5,13,7,15},{16,24,18,26,20,28,22,30},{17..., dimensions={0} | all-to-all | bytes 1572864 | tf_op jit(solution)/shard_map/all_to_all | solution.py:207
  68.0 5.2 %collective-permute-start.3 = (bf16[192,16,128]{2,1,0:T(8,128)(2,1)S(1)}, bf16[192,16,128]{2,1,0:T(8,128)(2,1)S(1)}, u32[]{:S(2)}, u32[]{:S(2)}) collective-permute-start(bf16[192,16,128]{2,1,0:T(8,128)(2,1)S(1)} %all_to_all.22.mine), channel_id=1, source_target_pairs={{0,1},{1,0},{2,3},{3,2},{4,5},{5,4},{6,7},{7,6},{8,9},{9,8},{10,11... | collective-permute-start | bytes 2359304 | tf_op jit(solution)/shard_map/ppermute | solution.py:257
  73.2 0.0 copy-done
  73.2 0.0 copy-done.1
  73.2 0.3 fusion.5.start
  73.5 1.6 %collective-permute-done.3.theirs = bf16[192,16,128]{2,1,0:T(8,128)(2,1)S(1)} collective-permute-done((bf16[192,16,128]{2,1,0:T(8,128)(2,1)S(1)}, bf16[192,16,128]{2,1,0:T(8,128)(2,1)S(1)}, u32[]{:S(2)}, u32[]{:S(2)}) %collective-permute-start.3) | collective-permute-done | bytes 786464 | tf_op jit(solution)/shard_map/ppermute | solution.py:257
  75.1 6.9 %backproject.1 = f32[64,16,128]{2,1,0:T(8,128)} custom-call(s32[1,2048]{1,0:T(1,128)} %pixels.3, s32[1,2048]{1,0:T(1,128)} %slots.3, s32[1,64]{1,0:T(1,128)} %counts.3, s32[5,64]{1,0:T(8,128)S(1)} %add_bitcast_fusion.owner_rows, s32[32]{0:T(128)} %subset.3, bf16[32,4,128,128]{3,2,1,0:T(8,128)(2,1)} %table.3, bf16[192,16,128]{2,1,0:T(8,128)(2,1)S(1)} %all_to_all.22.mine, ...), custom_call_target="tpu_custom_call" | custom-call | flops 1073741824 | bytes 6291456 | tf_op jit(solution)/shard_map/backproject/pallas_call | solution.py:162
  (6 shorter events, 0.1 us)
Async XLA Ops:
  8.5 5.2 %collective-permute-start = (bf16[192,16,128]{2,1,0:T(8,128)(2,1)S(1)}, bf16[192,16,128]{2,1,0:T(8,128)(2,1)S(1)}, u32[]{:S(2)}, u32[]{:S(2)}) collective-permute-start(bf16[192,16,128]{2,1,0:T(8,128)(2,1)S(1)} %get-tuple-element.10), channel_id=1, source_target_pairs={{0,1},{1,0},{2,3},{3,2},{4,5},{5,4},{6,7},{7,6},{8,9},{9,8},{10,11... | collective-permute-start | bytes 2359304 | tf_op jit(solution)/shard_map/ppermute | solution.py:243
  14.9 30.4 %copy-start.2 = (f32[6,16,128]{2,1,0:T(8,128)S(1)}, f32[6,16,128]{2,1,0:T(8,128)}, u32[]{:S(2)}) copy-start(f32[6,16,128]{2,1,0:T(8,128)} %param.19) | copy-start | bytes 147460
  14.9 30.4 %copy-start.3 = (f32[6,16,128]{2,1,0:T(8,128)S(1)}, f32[6,16,128]{2,1,0:T(8,128)}, u32[]{:S(2)}) copy-start(f32[6,16,128]{2,1,0:T(8,128)} %param.18) | copy-start | bytes 147460
  14.9 16.0 %all-to-all-start = ((bf16[192,16,128]{2,1,0:T(8,128)(2,1)}), bf16[192,16,128]{2,1,0:T(8,128)(2,1)S(1)}, u32[]{:S(2)}, u32[]{:S(2)}) async-start(bf16[192,16,128]{2,1,0:T(8,128)(2,1)} %add_convert_fusion), calls=%async_computation | async-start | bytes 1572864 | tf_op jit(solution)/shard_map/all_to_all | solution.py:207
  18.8 12.2 %collective-permute-start.1 = (f32[64,1,128]{2,1,0:T(1,128)S(1)}, f32[64,1,128]{2,1,0:T(1,128)S(1)}, u32[]{:S(2)}, u32[]{:S(2)}) collective-permute-start(f32[64,1,128]{2,1,0:T(1,128)S(1)} %get-tuple-element.11), channel_id=1, source_target_pairs={{0,64},{64,128},{128,192},{1,65},{65,129},{129,193},{2,66},{66,130... | collective-permute-start | bytes 98312 | tf_op jit(solution)/shard_map/ppermute | solution.py:244
  22.0 9.0 %collective-permute-start.2 = (f32[64,1,128]{2,1,0:T(1,128)S(1)}, f32[64,1,128]{2,1,0:T(1,128)S(1)}, u32[]{:S(2)}, u32[]{:S(2)}) collective-permute-start(f32[64,1,128]{2,1,0:T(1,128)S(1)} %get-tuple-element.12), channel_id=1, source_target_pairs={{64,0},{128,64},{192,128},{65,1},{129,65},{193,129},{66,2},{130,66... | collective-permute-start | bytes 98312 | tf_op jit(solution)/shard_map/ppermute | solution.py:245
  45.2 28.0 %copy-start = (f32[64,16,128]{2,1,0:T(8,128)S(1)}, f32[64,16,128]{2,1,0:T(8,128)}, u32[]{:S(2)}) copy-start(f32[64,16,128]{2,1,0:T(8,128)} %precond.1) | copy-start | bytes 1572868
  45.2 28.0 %copy-start.1 = (f32[64,16,128]{2,1,0:T(8,128)S(1)}, f32[64,16,128]{2,1,0:T(8,128)}, u32[]{:S(2)}) copy-start(f32[64,16,128]{2,1,0:T(8,128)} %image.1) | copy-start | bytes 1572868
  68.0 7.1 %collective-permute-start.3 = (bf16[192,16,128]{2,1,0:T(8,128)(2,1)S(1)}, bf16[192,16,128]{2,1,0:T(8,128)(2,1)S(1)}, u32[]{:S(2)}, u32[]{:S(2)}) collective-permute-start(bf16[192,16,128]{2,1,0:T(8,128)(2,1)S(1)} %all_to_all.22.mine), channel_id=1, source_target_pairs={{0,1},{1,0},{2,3},{3,2},{4,5},{5,4},{6,7},{7,6},{8,9},{9,8},{10,11... | collective-permute-start | bytes 2359304 | tf_op jit(solution)/shard_map/ppermute | solution.py:257
